TPU v7x, 256 devices: a whole 4x4x8 slice. The times are simulated.
256 devices in a mesh: row: 8 (over z_lo, y), col: 16 (over x, z_hi), rep: 2 (over core).
Axes of the slice: x: 4, y: 4, z: 8 (z_hi: 4, z_lo: 2; z = z_hi * 2 + z_lo), core: 2. Of those that a mesh axis runs over, the one named last changes fastest.
Arguments:
- streams: bfloat16 [16384, 4, 2048], P(('row', 'col', 'rep')), may hold values from -6 to 6
- lengths: int32 [8], P('row'), may hold values from 1 to 4096, as said below
- cache: bfloat16 [8, 16, 4096, 256], P('row', 'col', 'rep'), may hold values from -1000 to 1000, as said below
- hc_static: float32 [2, 4, 6], replicated, may hold values from -2 to 3
- hc_dynamic: bfloat16 [2, 2048, 6], replicated, may hold values from -0.125 to 0.125
- w_qkv: bfloat16 [2048, 16, 384], P('row', 'col'), may hold values from -0.125 to 0.125
- w_out: bfloat16 [2048, 2048], P('row', 'col'), may hold values from -0.125 to 0.125
- w_gate_up: bfloat16 [2048, 2, 8192], P('row', None, 'col'), may hold values from -0.125 to 0.125
- w_down: bfloat16 [2048, 8192], P('row', 'col'), may hold values from -0.0625 to 0.0625
Outputs:
- new_streams: bfloat16 [16384, 4, 2048], P(('row', 'col', 'rep'))
- decode_cache: bfloat16 [8, 2, 16, 2048, 256], P('row', None, 'rep', 'col')
- decode_new: bfloat16 [8, 2, 16, 1024, 256], P('row', None, 'rep', 'col')
Inputs may be any that keep to these rules, and one draw needn't show every extreme that they name: lengths[r] counts the valid cached positions of prompt r; in every draw one prompt's cache is full (4096 positions). cache positions at or after lengths[r] are not attended.
All inputs are finite; a program needn't handle non-finite values.
Results may differ from a plain program's by a relative error of at most 0.017.
Values may be sent and summed in bfloat16 or wider, within the bound.
A program may use at most 128 MiB of HBM per device.

v0:
```python
import math

import jax
import jax.numpy as jnp
from jax import lax
from jax.sharding import PartitionSpec as P

EPS = 1e-05
NEGATIVE = -1e30
FARAWAY = 1 << 30


def rotate(values, positions):
    rot_width = values.shape[-1]
    half_width = rot_width // 2
    inverse = jnp.exp(
        -jnp.log(10000.0) * (2.0 * jnp.arange(half_width, dtype=jnp.float32) / rot_width)
    )
    angles = positions.astype(jnp.float32)[:, None] * inverse[None, :]
    cosine = jnp.cos(angles)[:, None, :]
    sine_table = jnp.sin(angles)[:, None, :]
    first_half = values[..., :half_width]
    second = values[..., half_width:]
    return jnp.concatenate(
        [first_half * cosine - second * sine_table, second * cosine + first_half * sine_table],
        axis=-1,
    )


def connect(streams, static, dynamic):
    widened = streams.astype(jnp.float32)
    products = jnp.einsum("tsd,dk->tsk", streams, dynamic, preferred_element_type=jnp.float32)
    stream_rms = jnp.sqrt(jnp.mean(widened * widened, axis=2) + EPS)
    weights = static[None] + jnp.tanh(products / stream_rms[:, :, None])
    mixture = jnp.sum(weights[:, :, 0:1] * widened, axis=1)
    center = jnp.mean(mixture, axis=1, keepdims=True)
    spread = jnp.mean(mixture * mixture, axis=1, keepdims=True) - center * center
    normed = ((mixture - center) / jnp.sqrt(spread + EPS)).astype(jnp.bfloat16)
    return (weights, widened, normed)


def blend(weights, widened, branch):
    stream_count = widened.shape[1]
    outputs = []
    for target in range(stream_count):
        carried = jnp.sum(weights[:, :, 1 + target][:, :, None] * widened, axis=1)
        outputs.append(carried + weights[:, target, stream_count + 1][:, None] * branch)
    return jnp.stack(outputs, axis=1).astype(jnp.bfloat16)


def gather_input(normed):
    return lax.all_gather(normed, "col", axis=0, tiled=True)


def branch_sum(partial_terms):
    return lax.psum_scatter(
        partial_terms.astype(jnp.bfloat16), "col", scatter_dimension=0, tiled=True
    ).astype(jnp.float32)


def weight_rows(first_weight, second_weight):
    return (
        lax.all_gather(first_weight, "row", axis=0, tiled=True),
        lax.all_gather(second_weight, "row", axis=0, tiled=True),
    )


def fan_out(cache, fresh_kv):
    return (
        lax.all_to_all(
            lax.all_to_all(cache[:, None], "col", split_axis=3, concat_axis=2, tiled=True),
            "rep",
            split_axis=2,
            concat_axis=1,
            tiled=True,
        ),
        lax.all_to_all(
            lax.all_to_all(fresh_kv[None, None], "col", split_axis=3, concat_axis=2, tiled=True),
            "rep",
            split_axis=2,
            concat_axis=1,
            tiled=True,
        ),
    )


def on_device(streams, lengths, cache, hc_static, hc_dynamic, w_qkv, w_out, w_gate_up, w_down):
    col_count = lax.axis_size("col")
    rep_count = lax.axis_size("rep")
    rep_index = lax.axis_index("rep")
    tok_dev = streams.shape[0]
    tok_rep = tok_dev * col_count
    heads_here = w_qkv.shape[1]
    head_dim = w_qkv.shape[2] // 3
    cache_dev = cache.shape[2]
    span_rows = cache_dev + tok_rep
    length = lengths[0]
    mix_attn, wide_attn, normed_attn = connect(streams, hc_static[0], hc_dynamic[0])
    input_attn = gather_input(normed_attn)
    qkv_rows, out_rows = weight_rows(w_qkv, w_out)
    projected = jnp.dot(
        input_attn,
        qkv_rows.reshape(qkv_rows.shape[0], heads_here * 3 * head_dim),
        preferred_element_type=jnp.float32,
    )
    projected = projected.reshape(tok_rep, heads_here, 3 * head_dim)
    row_ids = jnp.arange(tok_rep, dtype=jnp.int32)
    stretch_ids = (row_ids // tok_dev * rep_count + rep_index) * tok_dev + row_ids % tok_dev
    query_pos = length + stretch_ids
    queries = jnp.transpose(
        rotate(projected[:, :, :head_dim], query_pos).astype(jnp.bfloat16), (1, 0, 2)
    )
    key_new = rotate(projected[:, :, head_dim : 2 * head_dim], query_pos).astype(jnp.bfloat16)
    value_new = projected[:, :, 2 * head_dim :].astype(jnp.bfloat16)
    fresh_kv = jnp.transpose(jnp.concatenate([key_new, value_new], axis=2), (1, 0, 2))
    own_keys = jnp.concatenate([cache[0], fresh_kv], axis=1)

    def make_attend(query_set, query_where):
        latest = jnp.max(query_where)

        def absorb(current, key_block, key_pos):
            running_max, running_sum, running_out = current
            scores = jnp.einsum(
                "hqd,hkd->hqk",
                query_set,
                key_block[:, :, :head_dim],
                preferred_element_type=jnp.float32,
            ) / math.sqrt(head_dim)
            allowed = key_pos[None, None, :] <= query_where[None, :, None]
            scores = jnp.where(allowed, scores, NEGATIVE)
            newest = jnp.maximum(running_max, jnp.max(scores, axis=2))
            factor = jnp.exp(running_max - newest)
            unnormed = jnp.where(allowed, jnp.exp(scores - newest[:, :, None]), 0.0)
            running_sum = running_sum * factor + jnp.sum(unnormed, axis=2)
            running_out = running_out * factor[:, :, None] + jnp.einsum(
                "hqk,hkd->hqd",
                unnormed.astype(jnp.bfloat16),
                key_block[:, :, head_dim:],
                preferred_element_type=jnp.float32,
            )
            return (newest, running_sum, running_out)

        def attend(carried, key_piece, first_row):
            piece_rows = key_piece.shape[1]
            block_rows = math.gcd(piece_rows, 512)

            def one_block(number, current):
                offset = number * block_rows
                key_block = lax.dynamic_slice_in_dim(key_piece, offset, block_rows, 1)
                global_row = offset + jnp.arange(block_rows, dtype=jnp.int32)
                owner_rep = global_row // span_rows
                within = global_row % span_rows
                cache_pos = owner_rep * cache_dev + within
                fresh_row = within - cache_dev
                fresh_ids = (
                    fresh_row // tok_dev * rep_count + owner_rep
                ) * tok_dev + fresh_row % tok_dev
                key_pos = jnp.where(
                    within < cache_dev,
                    jnp.where(cache_pos < length, cache_pos, FARAWAY),
                    length + fresh_ids,
                )
                return lax.cond(
                    jnp.min(key_pos) <= latest,
                    lambda inside: absorb(inside, key_block, key_pos),
                    lambda inside: inside,
                    current,
                )

            return lax.fori_loop(0, piece_rows // block_rows, one_block, carried)

        return attend

    initial = (
        jnp.full((heads_here, tok_rep), NEGATIVE, jnp.float32),
        jnp.zeros((heads_here, tok_rep), jnp.float32),
        jnp.zeros((heads_here, tok_rep, head_dim), jnp.float32),
    )
    running_max, running_sum, running_out = make_attend(queries, query_pos)(
        initial, lax.all_gather(own_keys, "rep", axis=1, tiled=True), jnp.int32(0)
    )
    attended = (running_out / running_sum[:, :, None]).astype(jnp.bfloat16)
    attended = jnp.transpose(attended, (1, 0, 2)).reshape(tok_rep, heads_here * head_dim)
    attn_partial = lax.dot_general(
        attended, out_rows, (((1,), (1,)), ((), ())), preferred_element_type=jnp.float32
    )
    attn_branch = branch_sum(attn_partial)
    streams_mid = blend(mix_attn, wide_attn, attn_branch)
    mix_ffn, wide_ffn, normed_ffn = connect(streams_mid, hc_static[1], hc_dynamic[1])
    input_ffn = gather_input(normed_ffn)
    gate_rows, down_rows = weight_rows(w_gate_up, w_down)
    gate_up = jnp.einsum("td,dkf->tkf", input_ffn, gate_rows, preferred_element_type=jnp.float32)
    hidden = (jax.nn.silu(gate_up[:, 0]) * gate_up[:, 1]).astype(jnp.bfloat16)
    ffn_partial = lax.dot_general(
        hidden, down_rows, (((1,), (1,)), ((), ())), preferred_element_type=jnp.float32
    )
    ffn_branch = branch_sum(ffn_partial)
    new_streams = blend(mix_ffn, wide_ffn, ffn_branch)
    decode_cache, decode_new = fan_out(cache, fresh_kv)
    return (new_streams, decode_cache, decode_new)


def solution(mesh):
    placed = (
        P(("row", "col", "rep"), None, None),
        P("row"),
        P("row", "col", "rep", None),
        P(),
        P(),
        P("row", "col", None),
        P("row", "col"),
        P("row", None, "col"),
        P("row", "col"),
    )
    return jax.shard_map(
        on_device,
        mesh=mesh,
        in_specs=placed,
        out_specs=(
            P(("row", "col", "rep"), None, None),
            P("row", None, "rep", "col", None),
            P("row", None, "rep", "col", None),
        ),
        check_vma=False,
    )
```

profile of v0, /device:TPU:34, one launch (start us, length us, event | category | flops | bytes accessed | tf_op | source)
XLA Modules:
  0.0 686.4 jit_solution(4608088730587352142)
XLA Ops:
  14.5 8.9 %fusion.43 = (f32[64]{0:T(128)S(1)}, f32[64,2048]{1,0:T(8,128)S(1)}, f32[64,2048]{1,0:T(8,128)}, f32[64,2048]{1,0:T(8,128)}, f32[64,2048]{1,0:T(8,128)}, /*index=5*/f32[64,2048]{1,0:T(8,128)}) fusion(bf16[64,4,2048]{2,1,0:T(4,128)(2,1)S(1)} %copy-done.1, f32[64,4]{1,0:T(8,128)S(1)} %copy.119, f32[64,4]{1,0:T(8,128)S(1)} %copy.118, f32[64,4]{1,0:T(8,128)S(1)} %copy.122, ...), kind=kLoop, calls=%fused_computation.80 | loop fusion | flops 5636032 | bytes 3675392 | tf_op jit(solution)/shard_map/reduce_sum | solution.py:36
  25.2 29.3 %all-gather.9.cloned.1.call-done = bf16[2048,1,384]{2,0,1:T(8,128)(2,1)} async-done(((bf16[256,1,384]{2,0,1:T(8,128)(2,1)}), bf16[2048,1,384]{2,0,1:T(8,128)(2,1)}) %all-gather.9.cloned.1.call-update) | async-done | bytes 1572880 | tf_op jit(solution)/shard_map/all_gather | solution.py:63
  54.5 80.2 %all-gather.7.cloned.1.call-done = bf16[1024,2048]{1,0:T(8,128)(2,1)} async-done(((bf16[64,2048]{1,0:T(8,128)(2,1)}), bf16[1024,2048]{1,0:T(8,128)(2,1)}) %all-gather.7.cloned.1.call-update) | async-done | bytes 4194320 | tf_op jit(solution)/shard_map/all_gather | solution.py:52
  134.7 4.5 fusion.59
  143.6 31.2 %all_gather.24 = bf16[2048,128]{1,0:T(8,128)(2,1)} all-gather(bf16[256,128]{1,0:T(8,128)(2,1)S(1)} %copy-done.9), channel_id=1, replica_groups=mesh['row'=8,'col'=16,'rep'=2] {'row'}, dimensions={0}, use_global_device_ids=true | all-gather | bytes 589824 | tf_op jit(solution)/shard_map/all_gather | solution.py:64
  175.8 75.6 %while.22 = (s32[]{:T(128)}, f32[1,1024]{1,0:T(1,128)S(1)}, f32[1,1024]{1,0:T(1,128)S(1)}, f32[1,1024,128]{2,1,0:T(8,128)}, s32[]{:T(128)}, /*index=5*/s32[]{:T(...) while((s32[]{:T(128)}, f32[1,1024]{1,0:T(1,128)S(1)}, ...), condition=%wide.region_12.13_spmd.clone.clone, body=%wide.region_6.12_spmd.clone.clone.sunk | while | flops 277129728 | bytes 8010217 | solution.py:170
  178.5 5.5 conditional.4
  181.2 2.7 fusion.5
  186.6 5.5 conditional.4
  189.3 2.7 fusion.5
  194.7 5.5 conditional.4
  197.4 2.7 fusion.5
  202.8 5.4 conditional.4
  210.9 5.5 conditional.4
  219.0 5.4 conditional.4
  237.9 5.5 conditional.4
  246.0 5.4 conditional.4
  251.4 4.5 convolution_convert_fusion.1
  258.2 111.9 %reduce-scatter.3.cloned.1.call-done = bf16[64,2048]{1,0:T(8,128)(2,1)} async-done(((bf16[1024,2048]{1,0:T(8,128)(2,1)}), bf16[64,2048]{1,0:T(8,128)(2,1)}) %reduce-scatter.3.cloned.1.call-update) | async-done | bytes 262160 | tf_op jit(solution)/shard_map/reduce_scatter | solution.py:56
  376.4 48.7 %all-gather.15.cloned.1.call-done = bf16[2048,2,512]{2,0,1:T(8,128)(2,1)} async-done(((bf16[256,2,512]{2,0,1:T(8,128)(2,1)}), bf16[2048,2,512]{2,0,1:T(8,128)(2,1)}) %all-gather.15.cloned.1.call-update) | async-done | bytes 4194320 | tf_op jit(solution)/shard_map/all_gather | solution.py:63
  425.1 80.4 %all-gather.13.cloned.1.call-done = bf16[1024,2048]{1,0:T(8,128)(2,1)} async-done(((bf16[64,2048]{1,0:T(8,128)(2,1)}), bf16[1024,2048]{1,0:T(8,128)(2,1)}) %all-gather.13.cloned.1.call-update) | async-done | bytes 4194320 | tf_op jit(solution)/shard_map/all_gather | solution.py:52
  505.5 9.9 %fusion.39 = f32[1024,2,512]{2,0,1:T(8,128)} fusion(bf16[2048,2,512]{2,0,1:T(8,128)(2,1)} %all-gather.15.cloned.1.call-done, bf16[1024,2048]{1,0:T(8,128)(2,1)} %all-gather.13.cloned.1.call-done), kind=kOutput, calls=%fused_computation.74 | convolution fusion | flops 4294967296 | bytes 12582912 | tf_op jit(solution)/shard_map/td,dkf->tkf/dot_general | solution.py:192
  515.5 33.3 %all-gather.17.cloned.1.call-done = bf16[2048,512]{1,0:T(8,128)(2,1)} async-done(((bf16[256,512]{1,0:T(8,128)(2,1)}), bf16[2048,512]{1,0:T(8,128)(2,1)}) %all-gather.17.cloned.1.call-update) | async-done | bytes 2097168 | tf_op jit(solution)/shard_map/all_gather | solution.py:64
  548.7 7.2 %convolution_convert_fusion = bf16[1024,2048]{1,0:T(8,128)(2,1)} fusion(bf16[2048,512]{1,0:T(8,128)(2,1)} %all-gather.17.cloned.1.call-done, f32[1024,2,512]{2,0,1:T(8,128)} %fusion.39), kind=kOutput, calls=%fused_computation.76 | convolution fusion | flops 2152726528 | bytes 10485760 | tf_op jit(solution)/shard_map/dot_general | solution.py:194
  555.9 11.7 %copy.143 = bf16[1,1,1,2048,256]{4,2,1,0,3:T(2,128)(2,1)S(1)} copy(bf16[1,1,1,2048,256]{4,3,2,1,0:T(8,128)(2,1)S(1)} %bitcast.156) | data formatting | bytes 2097152 | tf_op jit(solution)/shard_map/broadcast_in_dim | solution.py:71
  568.2 10.6 %reduce.8 = bf16[2048,256]{1,0:T(8,128)(2,1)S(1)} reduce(bf16[2048,1,1,1,256]{4,3,2,1,0:T(2,128)(2,1)S(1)} %bitcast.154, bf16[]{:T(256)} %broadcast.366), dimensions={1,2,3}, to_apply=%bitcast.150.reduce_sub_computation | reduce | bytes 2097154
  579.0 48.5 %all_to_all.48 = bf16[16,2,16384]{2,1,0:T(2,128)(2,1)S(1)} all-to-all(bf16[16,2,16384]{2,1,0:T(2,128)(2,1)S(1)} %reshape.308), channel_id=1, replica_groups=mesh['row'=8,'col'=16,'rep'=2] {'col'}, dimensions={0} | all-to-all | bytes 2097152 | tf_op jit(solution)/shard_map/all_to_all | solution.py:71
  629.8 3.6 all-to-all-start.1
  634.2 3.8 reduce.9
  639.0 7.8 %all-to-all-start.2 = ((bf16[16,2,8192]{2,1,0:T(2,128)(2,1)}), bf16[16,2,8192]{2,1,0:T(2,128)(2,1)S(1)}, u32[]{:S(2)}, u32[]{:S(2)}) async-start(bf16[16,2,8192]{2,1,0:T(2,128)(2,1)} %reshape.310), calls=%async_computation.4 | async-start | bytes 1048576 | tf_op jit(solution)/shard_map/all_to_all | solution.py:78
  646.8 21.0 %all-to-all-done.2 = bf16[16,2,8192]{2,1,0:T(2,128)(2,1)S(1)} async-done(((bf16[16,2,8192]{2,1,0:T(2,128)(2,1)}), bf16[16,2,8192]{2,1,0:T(2,128)(2,1)S(1)}, u32[]{:S(2)}, u32[]{:S(2)}) %all-to-all-start.2) | async-done | bytes 524320 | tf_op jit(solution)/shard_map/all_to_all | solution.py:78
  668.4 4.3 all_to_all.49
  (221 shorter events, 86.3 us)
Async XLA Ops:
  7.2 7.4 %copy-start.1 = (bf16[64,4,2048]{2,1,0:T(4,128)(2,1)S(1)}, bf16[64,4,2048]{2,1,0:T(4,128)(2,1)}, u32[]{:S(2)}) copy-start(bf16[64,4,2048]{2,1,0:T(4,128)(2,1)} %param.13) | copy-start | bytes 3145732
  7.2 47.3 %all-gather.9.cloned.1.call-start = ((), (), s32[]{:S(2)}) async-start(), calls=%async_computation.7 | async-start | bytes 1769472 | tf_op jit(solution)/shard_map/all_gather | solution.py:63
  7.9 126.8 %all-gather.7.cloned.1.call-start = ((), (), s32[]{:S(2)}) async-start(), calls=%async_computation.6 | async-start | bytes 4456448 | tf_op jit(solution)/shard_map/all_gather | solution.py:52
  24.4 150.6 %all-gather.11.cloned.1.call-start = ((), (), s32[]{:S(2)}) async-start(), calls=%async_computation.8 | async-start | bytes 4718592 | tf_op jit(solution)/shard_map/all_gather | solution.py:180
  139.2 2.4 copy-start
  141.6 1.9 copy-start.9
  142.9 227.1 %reduce-scatter.3.cloned.1.call-start = ((), (), s32[]{:S(2)}) async-start(), calls=%async_computation.9 | async-start | bytes 4456448 | tf_op jit(solution)/shard_map/reduce_scatter | solution.py:56
  255.9 114.1 %copy-start.5 = (f32[64,2048]{1,0:T(8,128)S(1)}, f32[64,2048]{1,0:T(8,128)}, u32[]{:S(2)}) copy-start(f32[64,2048]{1,0:T(8,128)} %get-tuple-element.576) | copy-start | bytes 1572868
  255.9 114.1 %copy-start.6 = (f32[64,2048]{1,0:T(8,128)S(1)}, f32[64,2048]{1,0:T(8,128)}, u32[]{:S(2)}) copy-start(f32[64,2048]{1,0:T(8,128)} %get-tuple-element.577) | copy-start | bytes 1572868
  255.9 114.1 %copy-start.7 = (f32[64,2048]{1,0:T(8,128)S(1)}, f32[64,2048]{1,0:T(8,128)}, u32[]{:S(2)}) copy-start(f32[64,2048]{1,0:T(8,128)} %get-tuple-element.578) | copy-start | bytes 1572868
  255.9 114.1 %copy-start.8 = (f32[64,2048]{1,0:T(8,128)S(1)}, f32[64,2048]{1,0:T(8,128)}, u32[]{:S(2)}) copy-start(f32[64,2048]{1,0:T(8,128)} %get-tuple-element.579) | copy-start | bytes 1572868
  255.9 169.2 %all-gather.15.cloned.1.call-start = ((), (), s32[]{:S(2)}) async-start(), calls=%async_computation.11 | async-start | bytes 4718592 | tf_op jit(solution)/shard_map/all_gather | solution.py:63
  258.1 247.4 %all-gather.13.cloned.1.call-start = ((), (), s32[]{:S(2)}) async-start(), calls=%async_computation.10 | async-start | bytes 4456448 | tf_op jit(solution)/shard_map/all_gather | solution.py:52
  375.4 173.3 %all-gather.17.cloned.1.call-start = ((), (), s32[]{:S(2)}) async-start(), calls=%async_computation.12 | async-start | bytes 2359296 | tf_op jit(solution)/shard_map/all_gather | solution.py:64
  376.2 298.2 %reduce-scatter.5.cloned.1.call-start = ((), (), s32[]{:S(2)}) async-start(), calls=%async_computation.13 | async-start | bytes 4456448 | tf_op jit(solution)/shard_map/reduce_scatter | solution.py:56
  628.6 4.7 copy-start.2
  629.8 9.2 %all-to-all-start.1 = ((bf16[1,1,16,128,256]{4,3,1,0,2:T(8,128)(2,1)}), bf16[1,1,16,128,256]{4,3,1,0,2:T(8,128)(2,1)S(1)}, u32[]{:S(2)}, u32[]{:S(2)}) async-start(bf16[1,1,16,128,256]{4,3,1,0,2:T(8,128)(2,1)} %bitcast.54), calls=%async_computation.3 | async-start | bytes 2097152 | tf_op jit(solution)/shard_map/all_to_all | solution.py:70
  639.0 28.8 %all-to-all-start.2 = ((bf16[16,2,8192]{2,1,0:T(2,128)(2,1)}), bf16[16,2,8192]{2,1,0:T(2,128)(2,1)S(1)}, u32[]{:S(2)}, u32[]{:S(2)}) async-start(bf16[16,2,8192]{2,1,0:T(2,128)(2,1)} %reshape.310), calls=%async_computation.4 | async-start | bytes 1048576 | tf_op jit(solution)/shard_map/all_to_all | solution.py:78
  646.8 27.6 %copy-start.3 = (f32[64,2048]{1,0:T(8,128)S(1)}, f32[64,2048]{1,0:T(8,128)}, u32[]{:S(2)}) copy-start(f32[64,2048]{1,0:T(8,128)} %get-tuple-element.572) | copy-start | bytes 1572868
  668.3 6.0 copy-start.4
Sparse Core Ops, SparseCore 0:
  9.8 44.6 all-gather.8
  56.9 77.7 all-gather.6
  143.0 15.7 all-gather.10
  256.0 113.9 reduce-scatter.2
  371.8 53.2 all-gather.14
  428.3 77.2 all-gather.12
  507.5 41.2 all-gather.16
  556.0 118.2 reduce-scatter.4
where the time goes:
time: 692 us; the launch traced here: 686 us
  waiting for transfers between devices  408 us (59%)
  blocking collectives  84 us (12%)
  other arithmetic  63.8 us (9%)
  matrix products  61.7 us (9%)
  local copies, waits for them, and re-layouts  26.4 us (4%)
  loops' own time  15.6 us (2%)
  between operations  15.1 us (2%)
  starting transfers between devices  11.9 us (2%)
    all_gather x2, waiting for transfers between devices, gather_input(): return lax.all_gather(normed, 'col', axis=0, tiled=True)  161 us
    reduce_scatter x2, waiting for transfers between devices, branch_sum(): lax.psum_scatter(partial_terms.astype(jnp.bfloat16), 'col', scatter_dimen...  113 us
    all_gather x2, waiting for transfers between devices, weight_rows(): lax.all_gather(first_weight, 'row', axis=0, tiled=True)  78 us
    all_to_all x1, blocking collectives, fan_out(): lax.all_to_all(cache[:, None], 'col', split_axis=3, concat_axis=2, tiled=...  48.5 us
    all_gather x1, waiting for transfers between devices, weight_rows(): lax.all_gather(second_weight, 'row', axis=0, tiled=True)  33.3 us
    all_gather x1, blocking collectives, weight_rows(): lax.all_gather(second_weight, 'row', axis=0, tiled=True)  31.2 us
    dot_general x8, matrix products, absorb(): jnp.einsum('hqk,hkd->hqd', unnormed.astype(jnp.bfloat16), key_block[:, :,...  21.8 us
    all_to_all x1, waiting for transfers between devices, fan_out(): lax.all_to_all(fresh_kv[None, None], 'col', split_axis=3, concat_axis=2,...  21 us
  transfers between devices with their start and end apart: 10, of which 8 were waited for; matrix products, arithmetic and copies ran while one was open for 10% of the time, Pallas kernels for 0%

commit v1 on v0

v1 whole, which is shorter than its diff:
```python
import functools
import math

import jax
import jax.numpy as jnp
from jax import lax
from jax.experimental import pallas as pl
from jax.experimental.pallas import tpu as pltpu
from jax.sharding import Mesh
from jax.sharding import PartitionSpec as P

EPS = 1e-05
NEGATIVE = -1e30
MESH = pl.DeviceIdType.MESH
ROW = ("zl", "y")
COL = ("x", "zh")
NX = 4
NZ = 4
BF = jnp.bfloat16
F32 = jnp.float32
VMEM_ALL = pl.BlockSpec(memory_space=pltpu.VMEM)
ANY = pl.BlockSpec(memory_space=pl.ANY)


def rope_tables(positions, rot_width):
    half_width = rot_width // 2
    inverse = jnp.exp(
        -jnp.log(10000.0) * (2.0 * jnp.arange(half_width, dtype=F32) / rot_width)
    )
    angles = positions.astype(F32)[:, None] * inverse[None, :]
    return jnp.cos(angles), jnp.sin(angles)


def rotate(values, cosine, sine):
    half_width = values.shape[-1] // 2
    first, second = values[:, :half_width], values[:, half_width:]
    return jnp.concatenate(
        [first * cosine - second * sine, second * cosine + first * sine], axis=-1
    )


def connect(streams, static, dynamic):
    widened = streams.astype(F32)
    products = jnp.einsum("tsd,dk->tsk", streams, dynamic, preferred_element_type=F32)
    stream_rms = jnp.sqrt(jnp.mean(widened * widened, axis=2) + EPS)
    weights = static[None] + jnp.tanh(products / stream_rms[:, :, None])
    mixture = jnp.sum(weights[:, :, 0:1] * widened, axis=1)
    center = jnp.mean(mixture, axis=1, keepdims=True)
    spread = jnp.mean(mixture * mixture, axis=1, keepdims=True) - center * center
    normed = ((mixture - center) / jnp.sqrt(spread + EPS)).astype(BF)
    return (weights, widened, normed)


def blend(weights, widened, branch):
    stream_count = widened.shape[1]
    outputs = []
    for target in range(stream_count):
        carried = jnp.sum(weights[:, :, 1 + target][:, :, None] * widened, axis=1)
        outputs.append(carried + weights[:, target, stream_count + 1][:, None] * branch)
    return jnp.stack(outputs, axis=1).astype(BF)


def around():
    x, z = lax.axis_index("x"), lax.axis_index("zh")
    return (
        x,
        z,
        lax.rem(x + 1, NX),
        lax.rem(x + NX - 1, NX),
        lax.rem(z + 1, NZ),
        lax.rem(z + NZ - 1, NZ),
    )


def greet(places):
    barrier = pltpu.get_barrier_semaphore()
    for place in places:
        pl.semaphore_signal(barrier, inc=1, device_id=place, device_id_type=MESH)
    pl.semaphore_wait(barrier, len(places))


def gather_kernel(t_ref, o_ref, send_sem, recv_sem, own_sem):
    x, z, xr, xl, zu, zd = around()
    right, left, up, down = {"x": xr}, {"x": xl}, {"zh": zu}, {"zh": zd}
    x2, z2 = lax.rem(x + 2, NX), lax.rem(z + 2, NZ)
    half = t_ref.shape[0] // 2
    top, low = pl.ds(0, half), pl.ds(half, half)
    whole = pl.ds(0, 2 * half)
    greet((right, left, up, down))

    def copy(kind, src, slot, rows, place):
        return pltpu.make_async_remote_copy(
            src_ref=src.at[rows],
            dst_ref=o_ref.at[slot, rows],
            send_sem=send_sem.at[kind],
            recv_sem=recv_sem.at[kind],
            device_id=place,
            device_id_type=MESH,
        )

    started = []

    def start(*given):
        made = copy(*given)
        made.start()
        started.append(made)

    mine = x * NZ + z

    def arrived(kind, slot, rows, place):
        copy(kind, t_ref, slot, rows, place).wait_recv()

    own = pltpu.make_async_copy(t_ref, o_ref.at[mine], own_sem)
    start(0, t_ref, mine, whole, up)
    start(1, t_ref, mine, whole, down)
    start(4, t_ref, mine, whole, right)
    start(5, t_ref, mine, whole, left)
    own.start()
    zs = (z, zd, zu, z2)
    below, above = x * NZ + zd, x * NZ + zu
    arrived(0, mine, whole, up)
    start(2, o_ref.at[below], below, top, up)
    start(8, o_ref.at[below], below, whole, right)
    start(9, o_ref.at[below], below, whole, left)
    arrived(1, mine, whole, down)
    start(3, o_ref.at[above], above, low, down)
    start(12, o_ref.at[above], above, whole, right)
    start(13, o_ref.at[above], above, whole, left)

    def relay(j):
        from_left, from_right = xl * NZ + zs[j], xr * NZ + zs[j]
        arrived(4 + 4 * j, mine, whole, right)
        start(6 + 4 * j, o_ref.at[from_left], from_left, top, right)
        arrived(5 + 4 * j, mine, whole, left)
        start(7 + 4 * j, o_ref.at[from_right], from_right, low, left)

    relay(0)
    far = x * NZ + z2
    arrived(2, mine, top, up)
    arrived(3, mine, low, down)
    start(16, o_ref.at[far], far, whole, right)
    start(17, o_ref.at[far], far, whole, left)
    relay(1)
    relay(2)
    relay(3)
    for j in range(4):
        arrived(6 + 4 * j, mine, top, right)
        arrived(7 + 4 * j, mine, low, left)
    own.wait()
    for made in started:
        made.wait_send()


def gather_tokens(block, number):
    rows, width = block.shape
    return pl.pallas_call(
        gather_kernel,
        out_shape=jax.ShapeDtypeStruct((NX * NZ, rows, width), BF),
        in_specs=[VMEM_ALL],
        out_specs=VMEM_ALL,
        scratch_shapes=[
            pltpu.SemaphoreType.DMA((20,)),
            pltpu.SemaphoreType.DMA((20,)),
            pltpu.SemaphoreType.DMA,
        ],
        compiler_params=pltpu.CompilerParams(
            collective_id=number, has_side_effects=True, vmem_limit_bytes=48 << 20
        ),
        name="gather_tokens",
    )(block)


def scatter_kernel(p_ref, o_ref, xin, xsum, tin, total, tsum, send_sem, recv_sem):
    x, z, xr, xl, zu, zd = around()
    right, left, up, down = {"x": xr}, {"x": xl}, {"zh": zu}, {"zh": zd}
    x2, z2 = lax.rem(x + 2, NX), lax.rem(z + 2, NZ)
    half = p_ref.shape[1] // 2
    top, low = pl.ds(0, half), pl.ds(half, half)
    greet((right, left, up, down))
    started = []

    def copy(kind, src, dst, place):
        return pltpu.make_async_remote_copy(
            src_ref=src,
            dst_ref=dst,
            send_sem=send_sem.at[kind],
            recv_sem=recv_sem.at[kind],
            device_id=place,
            device_id_type=MESH,
        )

    def start(*given):
        made = copy(*given)
        made.start()
        started.append(made)

    def arrived(kind, ref, place):
        copy(kind, ref, ref, place).wait_recv()

    zs = (z2, zu, zd, z)
    for j in range(4):
        far = x2 * NZ + zs[j]
        start(6 * j, p_ref.at[far, top], xin.at[j, 0], right)
        start(6 * j + 1, p_ref.at[far, low], xin.at[j, 1], left)
    for j in range(4):
        start(6 * j + 2, p_ref.at[xr * NZ + zs[j], low], xin.at[j, 2], right)
        start(6 * j + 3, p_ref.at[xl * NZ + zs[j], top], xin.at[j, 3], left)

    def wide(ref):
        return ref[...].astype(F32)

    for j in range(4):
        arrived(6 * j, xin.at[j, 0], right)
        xsum[j, 0] = (wide(p_ref.at[xr * NZ + zs[j], top]) + wide(xin.at[j, 0])).astype(BF)
        start(6 * j + 4, xsum.at[j, 0], xin.at[j, 4], right)
        arrived(6 * j + 1, xin.at[j, 1], left)
        xsum[j, 1] = (wide(p_ref.at[xl * NZ + zs[j], low]) + wide(xin.at[j, 1])).astype(BF)
        start(6 * j + 5, xsum.at[j, 1], xin.at[j, 5], left)

    def finish_x(j):
        for kind, place in ((2, right), (3, left), (4, right), (5, left)):
            arrived(6 * j + kind, xin.at[j, kind], place)
        here = x * NZ + zs[j]
        a = wide(p_ref.at[here, top]) + wide(xin.at[j, 4]) + wide(xin.at[j, 3])
        b = wide(p_ref.at[here, low]) + wide(xin.at[j, 2]) + wide(xin.at[j, 5])
        return a, b

    base = 24
    a, b = finish_x(0)
    total[0, 0], total[0, 1] = a.astype(BF), b.astype(BF)
    start(base, total.at[0, 0], tin.at[0], up)
    start(base + 1, total.at[0, 1], tin.at[1], down)
    a, b = finish_x(1)
    total[1, 1] = b.astype(BF)
    start(base + 2, total.at[1, 1], tin.at[2], up)
    arrived(base, tin.at[0], up)
    tsum[0] = (a + wide(tin.at[0])).astype(BF)
    start(base + 4, tsum.at[0], tin.at[4], up)
    a, b = finish_x(2)
    total[2, 0] = a.astype(BF)
    start(base + 3, total.at[2, 0], tin.at[3], down)
    arrived(base + 1, tin.at[1], down)
    tsum[1] = (b + wide(tin.at[1])).astype(BF)
    start(base + 5, tsum.at[1], tin.at[5], down)
    a, b = finish_x(3)
    for kind, place in ((2, up), (3, down), (4, up), (5, down)):
        arrived(base + kind, tin.at[kind], place)
    o_ref[top] = a + wide(tin.at[4]) + wide(tin.at[3])
    o_ref[low] = b + wide(tin.at[2]) + wide(tin.at[5])
    for made in started:
        made.wait_send()


def scatter_sum(partial, number):
    blocks, rows, width = partial.shape
    half = rows // 2
    return pl.pallas_call(
        scatter_kernel,
        out_shape=jax.ShapeDtypeStruct((rows, width), F32),
        in_specs=[VMEM_ALL],
        out_specs=VMEM_ALL,
        scratch_shapes=[
            pltpu.VMEM((4, 6, half, width), BF),
            pltpu.VMEM((4, 2, half, width), BF),
            pltpu.VMEM((6, half, width), BF),
            pltpu.VMEM((3, 2, half, width), BF),
            pltpu.VMEM((2, half, width), BF),
            pltpu.SemaphoreType.DMA((30,)),
            pltpu.SemaphoreType.DMA((30,)),
        ],
        compiler_params=pltpu.CompilerParams(
            collective_id=number, has_side_effects=True, vmem_limit_bytes=48 << 20
        ),
        name="scatter_sum",
    )(partial)


def decode_kernel(c_ref, f_ref, dc_ref, dn_ref, send_sem, recv_sem):
    x, z, e = lax.axis_index("x"), lax.axis_index("zh"), lax.axis_index("core")
    col = x * NZ + z
    count = NX * NZ
    per = dc_ref.shape[1]
    crows, frows = dc_ref.shape[2], dn_ref.shape[2]
    to_core, slot = col // per, lax.rem(col, per)
    barrier = pltpu.get_barrier_semaphore()

    def at(c, core):
        return {"x": c // NZ, "zh": lax.rem(c, NZ), "core": core}

    for s in range(per):
        source = e * per + lax.rem(slot + s, per)
        for core in range(2):

            @pl.when(jnp.logical_not(jnp.logical_and(source == col, e == core)))
            def _():
                pl.semaphore_signal(
                    barrier, inc=1, device_id=at(source, core), device_id_type=MESH
                )

    stays = (to_core == e).astype(jnp.int32)
    pl.semaphore_wait(barrier, count - stays)

    def pieces(c):
        return (
            (c_ref.at[pl.ds(pl.multiple_of(c * crows, crows), crows)], dc_ref.at[e, slot]),
            (f_ref.at[pl.ds(pl.multiple_of(c * frows, frows), frows)], dn_ref.at[e, slot]),
        )

    def remote(s, kind):
        c = lax.rem(col + s, count)
        src, dst = pieces(c)[kind]
        return pltpu.make_async_remote_copy(
            src_ref=src,
            dst_ref=dst,
            send_sem=send_sem.at[kind, s],
            recv_sem=recv_sem.at[kind, e, slot],
            device_id=at(c, to_core),
            device_id_type=MESH,
        )

    def local(kind):
        src, dst = pieces(col)[kind]
        return pltpu.make_async_copy(src, dst, send_sem.at[kind, 0])

    for s in range(1, count):
        for kind in range(2):
            remote(s, kind).start()
    for kind in range(2):

        @pl.when(to_core == e)
        def _():
            local(kind).start()

        @pl.when(to_core != e)
        def _():
            remote(0, kind).start()

    for core in range(2):
        for i in range(per):
            for kind, ref in ((0, dc_ref), (1, dn_ref)):

                @pl.when(jnp.logical_not(jnp.logical_and(core == e, e * per + i == col)))
                def _():
                    pltpu.make_async_remote_copy(
                        src_ref=ref.at[core, i],
                        dst_ref=ref.at[core, i],
                        send_sem=send_sem.at[kind, 0],
                        recv_sem=recv_sem.at[kind, core, i],
                        device_id=at(col, 1 - e),
                        device_id_type=MESH,
                    ).wait_recv()

    for s in range(1, count):
        for kind in range(2):
            remote(s, kind).wait_send()
    for kind in range(2):

        @pl.when(to_core == e)
        def _():
            local(kind).wait()

        @pl.when(to_core != e)
        def _():
            remote(0, kind).wait_send()


def decode_exchange(cache, fresh, number):
    count = NX * NZ
    per = count // 2
    (crows, width), frows = cache.shape, fresh.shape[0]
    return pl.pallas_call(
        decode_kernel,
        out_shape=(
            jax.ShapeDtypeStruct((2, per, crows // count, width), BF),
            jax.ShapeDtypeStruct((2, per, frows // count, width), BF),
        ),
        in_specs=[ANY, ANY],
        out_specs=(ANY, ANY),
        scratch_shapes=[
            pltpu.SemaphoreType.DMA((2, count)),
            pltpu.SemaphoreType.DMA((2, 2, per)),
        ],
        compiler_params=pltpu.CompilerParams(collective_id=number, has_side_effects=True),
        name="decode_exchange",
    )(cache, fresh)


SUB = 256
KEYS = 512


def attend_kernel(meta, q_ref, co_ref, cx_ref, fo_ref, fx_ref, o_ref, m_ref, l_ref, acc_ref):
    hd = q_ref.shape[1]
    subs = q_ref.shape[0] // SUB
    gain = 1.0 / (math.sqrt(hd) * math.log(2.0))
    length, rep = meta[0], meta[1]
    m_ref[...] = jnp.full_like(m_ref, NEGATIVE)
    l_ref[...] = jnp.zeros_like(l_ref)
    acc_ref[...] = jnp.zeros_like(acc_ref)

    def absorb(sub, keys, values, allowed):
        rows = pl.ds(sub * SUB, SUB)
        scores = lax.dot_general(
            q_ref[rows], keys, (((1,), (1,)), ((), ())), preferred_element_type=F32
        )
        if allowed is not None:
            scores = jnp.where(allowed, scores, NEGATIVE)
        before = m_ref[rows]
        newest = jnp.maximum(before, jnp.max(scores, axis=1, keepdims=True))
        factor = jnp.exp2((before - newest) * gain)
        probs = jnp.exp2((scores - newest[:, :1]) * gain)
        if allowed is not None:
            probs = jnp.where(allowed, probs, 0.0)
        m_ref[rows] = newest
        l_ref[rows] = l_ref[rows] * factor + jnp.sum(probs, axis=1, keepdims=True)
        acc_ref[rows] = acc_ref[rows] * factor + jnp.dot(
            probs.astype(BF), values, preferred_element_type=F32
        )

    def cached(ref, base):
        def one(number, unused):
            first = base + number * KEYS
            rows = pl.ds(pl.multiple_of(number * KEYS, KEYS), KEYS)

            @pl.when(first + KEYS <= length)
            def _():
                for sub in range(subs):
                    absorb(sub, ref[rows, :hd], ref[rows, hd:], None)

            @pl.when(jnp.logical_and(first < length, first + KEYS > length))
            def _():
                place = first + lax.broadcasted_iota(jnp.int32, (SUB, KEYS), 1)
                for sub in range(subs):
                    absorb(sub, ref[rows, :hd], ref[rows, hd:], place < length)

            return unused

        lax.fori_loop(0, ref.shape[0] // KEYS, one, 0)

    reach = co_ref.shape[0]
    cached(co_ref, rep * reach)
    cached(cx_ref, (1 - rep) * reach)
    tok = meta_tok(q_ref.shape[0])
    row = lax.broadcasted_iota(jnp.int32, (SUB, SUB), 0)
    column = lax.broadcasted_iota(jnp.int32, (SUB, SUB), 1)
    own_ok = column <= row
    other_ok = column // tok < row // tok + rep
    for number in range(subs):
        rows = pl.ds(number * SUB, SUB)
        for ref, allowed in ((fo_ref, own_ok), (fx_ref, other_ok)):
            for sub in range(number, subs):
                absorb(
                    sub, ref[rows, :hd], ref[rows, hd:], allowed if sub == number else None
                )
    o_ref[...] = (acc_ref[...] / l_ref[...]).astype(o_ref.dtype)


def meta_tok(rows):
    return rows // (NX * NZ)


def attend(meta, queries, cache_own, cache_other, fresh_own, fresh_other):
    rows, hd = queries.shape
    return pl.pallas_call(
        attend_kernel,
        out_shape=jax.ShapeDtypeStruct((rows, hd), BF),
        in_specs=[pl.BlockSpec(memory_space=pltpu.SMEM)] + [VMEM_ALL] * 5,
        out_specs=VMEM_ALL,
        scratch_shapes=[pltpu.VMEM((rows, hd), F32)] * 3,
        compiler_params=pltpu.CompilerParams(vmem_limit_bytes=48 << 20),
        cost_estimate=pl.CostEstimate(
            flops=4 * rows * hd * 5120,
            bytes_accessed=4 << 20,
            transcendentals=rows * 5120,
        ),
        name="attend",
    )(meta, queries, cache_own, cache_other, fresh_own, fresh_other)


def gather_rows(weight, rep_index):
    half = weight.shape[0] // 2
    mine = lax.dynamic_slice_in_dim(weight, rep_index * half, half, 0)
    return lax.all_gather(mine, ROW + ("core",), axis=0, tiled=True)


def swap(value):
    return lax.ppermute(value, "core", [(0, 1), (1, 0)])


def on_device(streams, lengths, cache, hc_static, hc_dynamic, w_qkv, w_out, w_gate_up, w_down):
    rep_count = 2
    col_count = NX * NZ
    rep_index = lax.axis_index("core")
    tok_dev, stream_count, width = streams.shape
    tok_rep = tok_dev * col_count
    head_dim = w_qkv.shape[2] // 3
    length = lengths[0]
    cache = cache[0, 0]
    cache_other = swap(cache)
    mix_attn, wide_attn, normed_attn = connect(streams, hc_static[0], hc_dynamic[0])
    input_attn = gather_tokens(normed_attn, 0).reshape(tok_rep, width)
    qkv_rows = gather_rows(w_qkv[:, 0, :], rep_index)
    projected = jnp.dot(input_attn, qkv_rows, preferred_element_type=F32)
    row_ids = jnp.arange(tok_rep, dtype=jnp.int32)
    stretch_ids = (row_ids // tok_dev * rep_count + rep_index) * tok_dev + row_ids % tok_dev
    cosine, sine = rope_tables(length + stretch_ids, head_dim)
    queries = rotate(projected[:, :head_dim], cosine, sine).astype(BF)
    key_new = rotate(projected[:, head_dim : 2 * head_dim], cosine, sine).astype(BF)
    value_new = projected[:, 2 * head_dim :].astype(BF)
    fresh = jnp.concatenate([key_new, value_new], axis=1)
    fresh_other = swap(fresh)
    meta = jnp.stack([length, rep_index])
    attended = attend(meta, queries, cache, cache_other, fresh, fresh_other)
    out_rows = gather_rows(w_out, rep_index)
    attn_partial = lax.dot_general(
        attended, out_rows, (((1,), (1,)), ((), ())), preferred_element_type=F32
    ).astype(BF)
    attn_branch = scatter_sum(attn_partial.reshape(col_count, tok_dev, width), 1)
    streams_mid = blend(mix_attn, wide_attn, attn_branch)
    mix_ffn, wide_ffn, normed_ffn = connect(streams_mid, hc_static[1], hc_dynamic[1])
    input_ffn = gather_tokens(normed_ffn, 2).reshape(tok_rep, width)
    gate_rows = gather_rows(w_gate_up, rep_index)
    down_rows = gather_rows(w_down, rep_index)
    gate_up = jnp.einsum("td,dkf->tkf", input_ffn, gate_rows, preferred_element_type=F32)
    hidden = (jax.nn.silu(gate_up[:, 0]) * gate_up[:, 1]).astype(BF)
    ffn_partial = lax.dot_general(
        hidden, down_rows, (((1,), (1,)), ((), ())), preferred_element_type=F32
    ).astype(BF)
    ffn_branch = scatter_sum(ffn_partial.reshape(col_count, tok_dev, width), 3)
    new_streams = blend(mix_ffn, wide_ffn, ffn_branch)
    decode_cache, decode_new = decode_exchange(cache, fresh, 4)
    return (new_streams, decode_cache[None], decode_new[None])


def solution(mesh):
    rows = mesh.devices.shape[0]
    fine = Mesh(
        mesh.devices.reshape((2, rows // 2, NX, NZ, 2)), ("zl", "y", "x", "zh", "core")
    )
    placed = (
        P(ROW + COL + ("core",), None, None),
        P(ROW),
        P(ROW, COL, "core", None),
        P(),
        P(),
        P(ROW, COL, None),
        P(ROW, COL),
        P(ROW, None, COL),
        P(ROW, COL),
    )
    return jax.shard_map(
        on_device,
        mesh=fine,
        in_specs=placed,
        out_specs=(
            P(ROW + COL + ("core",), None, None),
            P(ROW, None, "core", COL, None),
            P(ROW, None, "core", COL, None),
        ),
        check_vma=False,
    )
```

time: 692 us -> 360 us (0.52)
  waiting for transfers between devices: 408 us -> 0.08 us
  Pallas kernels: 0 us -> 254 us
  blocking collectives: 84 us -> 30.9 us
  other arithmetic: 63.8 us -> 16.7 us
  matrix products: 61.7 us -> 23.2 us
  loops' own time: 15.6 us -> 0 us
  local copies, waits for them, and re-layouts: 26.4 us -> 13.4 us
  starting transfers between devices: 11.9 us -> 0.31 us
    all_gather x6 -> x3, waiting for transfers between devices: 272 us -> 0.02 us  [gather_rows(): return lax.all_gather(mine, ROW + ('core',), axis=0, tiled=True)]
    pallas_call x0 -> x6, Pallas kernels: none -> 254 us  [the longest x2 93.3 us: gather_tokens(): pl.pallas_call(gather_kernel, out_shape=jax.ShapeDtypeStruct((NX * NZ, ro...]
    reduce_scatter x2 -> x0, waiting for transfers between devices: 113 us -> none  [branch_sum(): lax.psum_scatter(partial_terms.astype(jnp.bfloat16), 'col', scatter_dimen...]
    all_to_all x2 -> x0, blocking collectives: 52.8 us -> none  [the longest x1 48.5 us: fan_out(): lax.all_to_all(cache[:, None], 'col', split_axis=3, concat_axis=2, tiled=...]
    dot_general x20 -> x4, matrix products: 50.1 us -> 16.7 us  [the longest x1 9.92 us: on_device(): jnp.einsum('td,dkf->tkf', input_ffn, gate_rows, preferred_element_type=F32)]
    all_to_all x2 -> x0, waiting for transfers between devices: 21 us -> none  [the longest x1 21 us: fan_out(): lax.all_to_all(fresh_kv[None, None], 'col', split_axis=3, concat_axis=2,...]
    select_n x12 -> x0, other arithmetic: 16.6 us -> none  [one_block(): jnp.where(within < cache_dev, jnp.where(cache_pos < length, cache_pos, FA...]
    another operation x13 -> x0, loops' own time: 15.6 us -> none  [the longest x1 15.1 us: attend(): return lax.fori_loop(0, piece_rows // block_rows, one_block, carried)]
  transfers between devices with their start and end apart: 10 -> 5, of which waited for: 8 -> 0; matrix products, arithmetic and copies ran while one was open for 10% -> 11% of each run, Pallas kernels for 0% -> 59%
where the time goes in v1:
time: 360 us; the launch traced here: 354 us
  Pallas kernels  254 us (71%)
  blocking collectives  30.9 us (9%)
  matrix products  23.2 us (6%)
  other arithmetic  16.7 us (5%)
  between operations  14.8 us (4%)
  local copies, waits for them, and re-layouts  13.4 us (4%)
    pallas_call x2, Pallas kernels, gather_tokens(): pl.pallas_call(gather_kernel, out_shape=jax.ShapeDtypeStruct((NX * NZ, ro...  93.3 us
    pallas_call x2, Pallas kernels, scatter_sum(): pl.pallas_call(scatter_kernel, out_shape=jax.ShapeDtypeStruct((rows, widt...  90.9 us
    pallas_call x1, Pallas kernels, decode_exchange(): pl.pallas_call(decode_kernel, out_shape=(jax.ShapeDtypeStruct((2, per, cr...  47 us
    all_gather x1, blocking collectives, gather_rows(): return lax.all_gather(mine, ROW + ('core',), axis=0, tiled=True)  30.9 us
    pallas_call x1, Pallas kernels, attend(): pl.pallas_call(attend_kernel, out_shape=jax.ShapeDtypeStruct((rows, hd),...  23.1 us
    reduce_sum x2, other arithmetic, connect(): center = jnp.mean(mixture, axis=1, keepdims=True)  9.96 us
    dot_general x1, matrix products, on_device(): jnp.einsum('td,dkf->tkf', input_ffn, gate_rows, preferred_element_type=F32)  9.92 us
    unnamed x38, local copies, waits for them, and re-layouts  9.32 us
  transfers between devices with their start and end apart: 5, of which 0 were waited for; matrix products, arithmetic and copies ran while one was open for 11% of the time, Pallas kernels for 59%

profile of v1, /device:TPU:34, one launch (start us, length us, event | category | flops | bytes accessed | tf_op | source)
XLA Modules:
  0.0 353.7 jit_solution(13422976079040087738)
XLA Ops:
  7.3 1.6 constant_dynamic-slice_fusion.3
  9.0 0.2 constant_dynamic-slice_fusion.1
  9.2 0.7 copy.84
  10.1 1.6 constant_dynamic-slice_fusion
  11.8 0.6 fusion.4
  12.5 1.2 fusion.21
  14.3 8.9 %fusion.2 = (f32[64]{0:T(128)S(1)}, f32[64,2048]{1,0:T(8,128)S(1)}, f32[64,2048]{1,0:T(8,128)}, f32[64,2048]{1,0:T(8,128)}, f32[64,2048]{1,0:T(8,128)}, /*index=5*/f32[64,2048]{1,0:T(8,128)}) fusion(bf16[64,4,2048]{2,1,0:T(4,128)(2,1)S(1)} %copy-done.6, f32[64,4]{1,0:T(8,128)S(1)} %copy.68, f32[64,4]{1,0:T(8,128)S(1)} %copy.67, f32[64,4]{1,0:T(8,128)S(1)} %copy.75, ...), kind=kLoop, calls=%fused_computation.16 | loop fusion | flops 5636032 | bytes 3675392 | tf_op jit(solution)/shard_map/reduce_sum | solution.py:48
  23.4 49.2 %gather_tokens.2 = bf16[16,64,2048]{2,1,0:T(8,128)(2,1)S(1)} custom-call(bf16[64,2048]{1,0:T(8,128)(2,1)S(1)} %divide_convert_fusion.1.t_ref), custom_call_target="tpu_custom_call" | custom-call | tf_op jit(solution)/shard_map/gather_tokens/pallas_call | solution.py:156
  72.6 2.0 copy-done.2
  75.3 5.0 %fusion.16 = f32[1024,384]{1,0:T(8,128)S(1)} fusion(bf16[1024,2048]{1,0:T(8,128)(2,1)} %bitcast.91, bf16[2048,1,384]{2,0,1:T(8,128)(2,1)} %all-gather.9.cloned.1.call-done), kind=kOutput, calls=%fused_computation.32 | convolution fusion | flops 1610612736 | bytes 7340032 | tf_op jit(solution)/shard_map/dot_general | solution.py:503
  80.4 3.1 fusion.38
  83.5 0.2 pad_maximum_fusion.2.fo_ref.f_ref
  84.0 30.9 %all_gather.13 = bf16[2048,128]{1,0:T(8,128)(2,1)} all-gather(bf16[128,128]{1,0:T(8,128)(2,1)S(1)} %constant_dynamic-slice_fusion.2), channel_id=1, replica_groups=mesh['zl'=2,'y'=4,'x'=4,'zh'=4,'core'=2] {'zl','y','core'}, dimensions={0}, use_global_device_ids=true | all-gather | bytes 557056 | tf_op jit(solution)/shard_map/all_gather | solution.py:483
  114.9 47.0 %decode_exchange.1 = (bf16[2,8,128,256]{3,2,1,0:T(8,128)(2,1)}, bf16[2,8,64,256]{3,2,1,0:T(8,128)(2,1)}) custom-call(bf16[2048,256]{1,0:T(8,128)(2,1)} %bitcast.93, bf16[1024,256]{1,0:T(8,128)(2,1)} %copy-done.3), custom_call_target="tpu_custom_call" | custom-call | tf_op jit(solution)/shard_map/decode_exchange/pallas_call | solution.py:371
  161.9 1.2 pad_maximum_fusion.3.q_ref
  163.1 1.0 copy-done.4
  164.1 23.1 %attend.1 = bf16[1024,128]{1,0:T(8,128)(2,1)S(1)} custom-call(s32[2]{0:T(128)S(1)} %pad_add_fusion.meta, bf16[1024,128]{1,0:T(8,128)(2,1)S(1)} %pad_maximum_fusion.3.q_ref, bf16[2048,256]{1,0:T(8,128)(2,1)S(1)} %bitcast.94, bf16[2048,256]{1,0:T(8,128)(2,1)S(1)} %collective-permute-done.cx_ref, bf16[1024,256]{1,0:T(8,128)(2,1)S(1)} %copy-done.4, ...), custom_call_target="tpu_custom_call" | custom-call | flops 2684354560 | bytes 4194304 | tf_op jit(solution)/shard_map/attend/pallas_call | solution.py:464
  187.2 1.3 convolution_convert_fusion.1
  188.5 44.4 %scatter_sum.2 = f32[64,2048]{1,0:T(8,128)S(1)} custom-call(bf16[16,64,2048]{2,1,0:T(8,128)(2,1)S(1)} %bitcast.88), custom_call_target="tpu_custom_call" | custom-call | tf_op jit(solution)/shard_map/scatter_sum/pallas_call | solution.py:257
  232.9 0.3 fusion.41
  233.1 0.3 fusion.9
  233.5 0.5 fusion.19
  234.0 1.1 fusion
  235.4 44.1 %gather_tokens.3 = bf16[16,64,2048]{2,1,0:T(8,128)(2,1)S(1)} custom-call(bf16[64,2048]{1,0:T(8,128)(2,1)S(1)} %divide_convert_fusion.t_ref), custom_call_target="tpu_custom_call" | custom-call | tf_op jit(solution)/shard_map/gather_tokens/pallas_call | solution.py:156
  279.5 2.0 copy-done.1
  281.5 9.9 %fusion.66 = f32[1024,2,512]{2,0,1:T(8,128)} fusion(bf16[1024,2048,1]{1,0,2:T(8,128)(2,1)} %bitcast.90, bf16[2048,2,512]{2,0,1:T(8,128)(2,1)} %all-gather.5.cloned.1.call-done), kind=kOutput, calls=%fused_computation.130 | convolution fusion | flops 4294967296 | bytes 12582912 | tf_op jit(solution)/shard_map/td,dkf->tkf/dot_general | solution.py:524
  291.4 5.2 %convolution_convert_fusion = bf16[1024,2048]{1,0:T(8,128)(2,1)S(1)} fusion(bf16[2048,512]{1,0:T(8,128)(2,1)} %all-gather.7.cloned.1.call-done, f32[1024,2,512]{2,0,1:T(8,128)} %fusion.66), kind=kOutput, calls=%fused_computation.12 | convolution fusion | flops 2152726528 | bytes 10485760 | tf_op jit(solution)/shard_map/dot_general | solution.py:526
  296.6 46.6 %scatter_sum.3 = f32[64,2048]{1,0:T(8,128)S(1)} custom-call(bf16[16,64,2048]{2,1,0:T(8,128)(2,1)S(1)} %bitcast.89), custom_call_target="tpu_custom_call" | custom-call | tf_op jit(solution)/shard_map/scatter_sum/pallas_call | solution.py:257
  343.2 0.2 fusion.45
  343.6 1.8 copy.80
  345.4 1.0 copy.94
  346.4 0.8 copy.95
  (70 shorter events, 2.0 us)
Async XLA Ops:
  7.2 1.8 copy-start
  7.2 4.5 %copy-start.14 = (bf16[2,2048,6]{1,0,2:T(2,128)(2,1)S(1)}, bf16[2,2048,6]{1,0,2:T(2,128)(2,1)}, u32[]{:S(2)}) copy-start(bf16[2,2048,6]{1,0,2:T(2,128)(2,1)} %param.13) | copy-start | bytes 147460
  7.2 4.6 %copy-start.16 = (f32[2,4,6]{2,1,0:T(4,128)S(1)}, f32[2,4,6]{2,1,0:T(4,128)}, u32[]{:S(2)}) copy-start(f32[2,4,6]{2,1,0:T(4,128)} %param.12) | copy-start | bytes 580
  7.2 4.6 %copy-start.6 = (bf16[64,4,2048]{2,1,0:T(4,128)(2,1)S(1)}, bf16[64,4,2048]{2,1,0:T(4,128)(2,1)}, u32[]{:S(2)}) copy-start(bf16[64,4,2048]{2,1,0:T(4,128)(2,1)} %param.9) | copy-start | bytes 3145732
  7.2 68.1 %all-gather.9.cloned.1.call-start = ((), (), s32[]{:S(2)}) async-start(), calls=%async_computation.2 | async-start | bytes 1671168 | tf_op jit(solution)/shard_map/all_gather | solution.py:483
  8.9 272.5 %all-gather.5.cloned.1.call-start = ((), (), s32[]{:S(2)}) async-start(), calls=%async_computation | async-start | bytes 4456448 | tf_op jit(solution)/shard_map/all_gather | solution.py:483
  9.9 281.4 %all-gather.7.cloned.1.call-start = ((), (), s32[]{:S(2)}) async-start(), calls=%async_computation.1 | async-start | bytes 2228224 | tf_op jit(solution)/shard_map/all_gather | solution.py:483
  10.0 153.0 %collective-permute-start = (bf16[2048,256]{1,0:T(8,128)(2,1)}, bf16[2048,256]{1,0:T(8,128)(2,1)S(1)}, u32[]{:S(2)}, u32[]{:S(2)}) collective-permute-start(bf16[2048,256]{1,0:T(8,128)(2,1)} %bitcast.92), channel_id=1, source_target_pairs={{0,1},{1,0},{2,3},{3,2},{4,5},{5,4},{6,7},{7,6},{8,9},{9,8},{10,11... | collective-permute-start | bytes 3145736 | tf_op jit(solution)/shard_map/ppermute | solution.py:487
  72.6 2.0 copy-start.2
  80.4 3.6 %copy-start.15 = (bf16[256,128]{1,0:T(8,128)(2,1)S(1)}, bf16[256,128]{1,0:T(8,128)(2,1)}, u32[]{:S(2)}) copy-start(bf16[256,128]{1,0:T(8,128)(2,1)} %param.15) | copy-start | bytes 196612
  83.5 79.5 %copy-start.5 = (bf16[1,1,2048,256]{3,2,1,0:T(8,128)(2,1)S(1)}, bf16[1,1,2048,256]{3,2,1,0:T(8,128)(2,1)}, u32[]{:S(2)}) copy-start(bf16[1,1,2048,256]{3,2,1,0:T(8,128)(2,1)} %param.11) | copy-start | bytes 3145732
  83.8 31.1 %copy-start.3 = (bf16[1024,256]{1,0:T(8,128)(2,1)}, bf16[1024,256]{1,0:T(8,128)(2,1)S(1)}, u32[]{:S(2)}) copy-start(bf16[1024,256]{1,0:T(8,128)(2,1)S(1)} %pad_maximum_fusion.2.fo_ref.f_ref) | copy-start | bytes 1572868
  83.8 79.3 %collective-permute-start.1 = (bf16[1024,256]{1,0:T(8,128)(2,1)S(1)}, bf16[1024,256]{1,0:T(8,128)(2,1)}, u32[]{:S(2)}, u32[]{:S(2)}) collective-permute-start(bf16[1024,256]{1,0:T(8,128)(2,1)S(1)} %pad_maximum_fusion.2.fo_ref.f_ref), channel_id=1, source_target_pairs={{0,1},{1,0},{2,3},{3,2},{4,5},{5,4},{6,7},{7,6},{8,9},{9,8},{10,11... | collective-permute-start | bytes 1572872 | tf_op jit(solution)/shard_map/ppermute | solution.py:487
  161.9 25.3 %copy-start.7 = (bf16[2048,128]{1,0:T(8,128)(2,1)S(1)}, bf16[2048,128]{1,0:T(8,128)(2,1)}, u32[]{:S(2)}) copy-start(bf16[2048,128]{1,0:T(8,128)(2,1)} %all_gather.13) | copy-start | bytes 1572868
  163.1 1.0 copy-start.4
  188.4 44.4 %copy-start.8 = (f32[64,2048]{1,0:T(8,128)S(1)}, f32[64,2048]{1,0:T(8,128)}, u32[]{:S(2)}) copy-start(f32[64,2048]{1,0:T(8,128)} %get-tuple-element.27) | copy-start | bytes 1572868
  188.4 44.4 %copy-start.9 = (f32[64,2048]{1,0:T(8,128)S(1)}, f32[64,2048]{1,0:T(8,128)}, u32[]{:S(2)}) copy-start(f32[64,2048]{1,0:T(8,128)} %get-tuple-element.28) | copy-start | bytes 1572868
  188.5 44.4 %copy-start.10 = (f32[64,2048]{1,0:T(8,128)S(1)}, f32[64,2048]{1,0:T(8,128)}, u32[]{:S(2)}) copy-start(f32[64,2048]{1,0:T(8,128)} %get-tuple-element.29) | copy-start | bytes 1572868
  188.5 44.4 %copy-start.11 = (f32[64,2048]{1,0:T(8,128)S(1)}, f32[64,2048]{1,0:T(8,128)}, u32[]{:S(2)}) copy-start(f32[64,2048]{1,0:T(8,128)} %get-tuple-element.30) | copy-start | bytes 1572868
  279.5 2.0 copy-start.1
  343.5 1.9 copy-start.12
  343.6 2.8 copy-start.13
Sparse Core Ops, SparseCore 0:
  9.9 45.2 all-gather.8
  57.0 41.1 all-gather.4
  100.0 49.8 all-gather.6

commit v2 on v1

--- a/solution.py
+++ b/solution.py
@@ -5,6 +5,7 @@
 import jax.numpy as jnp
 from jax import lax
 from jax.experimental import pallas as pl
+from jax.experimental.layout import Layout, with_layout_constraint
 from jax.experimental.pallas import tpu as pltpu
 from jax.sharding import Mesh
 from jax.sharding import PartitionSpec as P
@@ -41,23 +42,24 @@
 
 def connect(streams, static, dynamic):
     widened = streams.astype(F32)
-    products = jnp.einsum("tsd,dk->tsk", streams, dynamic, preferred_element_type=F32)
+    products = jnp.einsum("std,dk->stk", streams, dynamic, preferred_element_type=F32)
     stream_rms = jnp.sqrt(jnp.mean(widened * widened, axis=2) + EPS)
-    weights = static[None] + jnp.tanh(products / stream_rms[:, :, None])
-    mixture = jnp.sum(weights[:, :, 0:1] * widened, axis=1)
+    weights = static[:, None] + jnp.tanh(products / stream_rms[:, :, None])
+    mixture = jnp.sum(weights[:, :, 0:1] * widened, axis=0)
     center = jnp.mean(mixture, axis=1, keepdims=True)
     spread = jnp.mean(mixture * mixture, axis=1, keepdims=True) - center * center
     normed = ((mixture - center) / jnp.sqrt(spread + EPS)).astype(BF)
-    return (weights, widened, normed)
-
-
-def blend(weights, widened, branch):
-    stream_count = widened.shape[1]
+    return (weights, normed)
+
+
+def blend(weights, streams, branch):
+    stream_count = streams.shape[0]
+    widened = streams.astype(F32)
     outputs = []
     for target in range(stream_count):
-        carried = jnp.sum(weights[:, :, 1 + target][:, :, None] * widened, axis=1)
-        outputs.append(carried + weights[:, target, stream_count + 1][:, None] * branch)
-    return jnp.stack(outputs, axis=1).astype(BF)
+        carried = jnp.sum(weights[:, :, 1 + target][:, :, None] * widened, axis=0)
+        outputs.append(carried + weights[target, :, stream_count + 1][:, None] * branch)
+    return jnp.stack(outputs, axis=0).astype(BF)
 
 
 def around():
@@ -275,7 +277,7 @@
     )(partial)
 
 
-def decode_kernel(c_ref, f_ref, dc_ref, dn_ref, send_sem, recv_sem):
+def decode_copies(c_ref, f_ref, dc_ref, dn_ref, send_sem, recv_sem):
     x, z, e = lax.axis_index("x"), lax.axis_index("zh"), lax.axis_index("core")
     col = x * NZ + z
     count = NX * NZ
@@ -335,6 +337,7 @@
         def _():
             remote(0, kind).start()
 
+    yield
     for core in range(2):
         for i in range(per):
             for kind, ref in ((0, dc_ref), (1, dn_ref)):
@@ -364,36 +367,20 @@
             remote(0, kind).wait_send()
 
 
-def decode_exchange(cache, fresh, number):
-    count = NX * NZ
-    per = count // 2
-    (crows, width), frows = cache.shape, fresh.shape[0]
-    return pl.pallas_call(
-        decode_kernel,
-        out_shape=(
-            jax.ShapeDtypeStruct((2, per, crows // count, width), BF),
-            jax.ShapeDtypeStruct((2, per, frows // count, width), BF),
-        ),
-        in_specs=[ANY, ANY],
-        out_specs=(ANY, ANY),
-        scratch_shapes=[
-            pltpu.SemaphoreType.DMA((2, count)),
-            pltpu.SemaphoreType.DMA((2, 2, per)),
-        ],
-        compiler_params=pltpu.CompilerParams(collective_id=number, has_side_effects=True),
-        name="decode_exchange",
-    )(cache, fresh)
-
-
 SUB = 256
 KEYS = 512
 
 
-def attend_kernel(meta, q_ref, co_ref, cx_ref, fo_ref, fx_ref, o_ref, m_ref, l_ref, acc_ref):
+def attend_kernel(
+    meta, q_ref, co_ref, cx_ref, fo_ref, fx_ref, o_ref, dc_ref, dn_ref,
+    m_ref, l_ref, acc_ref, send_sem, recv_sem,
+):
     hd = q_ref.shape[1]
     subs = q_ref.shape[0] // SUB
     gain = 1.0 / (math.sqrt(hd) * math.log(2.0))
-    length, rep = meta[0], meta[1]
+    length, rep = meta[0], lax.axis_index("core")
+    copies = decode_copies(co_ref, fo_ref, dc_ref, dn_ref, send_sem, recv_sem)
+    next(copies)
     m_ref[...] = jnp.full_like(m_ref, NEGATIVE)
     l_ref[...] = jnp.zeros_like(l_ref)
     acc_ref[...] = jnp.zeros_like(acc_ref)
@@ -421,18 +408,9 @@
         def one(number, unused):
             first = base + number * KEYS
             rows = pl.ds(pl.multiple_of(number * KEYS, KEYS), KEYS)
-
-            @pl.when(first + KEYS <= length)
-            def _():
-                for sub in range(subs):
-                    absorb(sub, ref[rows, :hd], ref[rows, hd:], None)
-
-            @pl.when(jnp.logical_and(first < length, first + KEYS > length))
-            def _():
-                place = first + lax.broadcasted_iota(jnp.int32, (SUB, KEYS), 1)
-                for sub in range(subs):
-                    absorb(sub, ref[rows, :hd], ref[rows, hd:], place < length)
-
+            place = first + lax.broadcasted_iota(jnp.int32, (SUB, KEYS), 1)
+            for sub in range(subs):
+                absorb(sub, ref[rows, :hd], ref[rows, hd:], place < length)
             return unused
 
         lax.fori_loop(0, ref.shape[0] // KEYS, one, 0)
@@ -453,21 +431,36 @@
                     sub, ref[rows, :hd], ref[rows, hd:], allowed if sub == number else None
                 )
     o_ref[...] = (acc_ref[...] / l_ref[...]).astype(o_ref.dtype)
+    for _ in copies:
+        pass
 
 
 def meta_tok(rows):
     return rows // (NX * NZ)
 
 
-def attend(meta, queries, cache_own, cache_other, fresh_own, fresh_other):
+def attend(meta, queries, cache_own, cache_other, fresh_own, fresh_other, number):
     rows, hd = queries.shape
+    count = NX * NZ
+    per = count // 2
+    (crows, width), frows = cache_own.shape, fresh_own.shape[0]
     return pl.pallas_call(
         attend_kernel,
-        out_shape=jax.ShapeDtypeStruct((rows, hd), BF),
+        out_shape=(
+            jax.ShapeDtypeStruct((rows, hd), BF),
+            jax.ShapeDtypeStruct((2, per, crows // count, width), BF),
+            jax.ShapeDtypeStruct((2, per, frows // count, width), BF),
+        ),
         in_specs=[pl.BlockSpec(memory_space=pltpu.SMEM)] + [VMEM_ALL] * 5,
-        out_specs=VMEM_ALL,
-        scratch_shapes=[pltpu.VMEM((rows, hd), F32)] * 3,
-        compiler_params=pltpu.CompilerParams(vmem_limit_bytes=48 << 20),
+        out_specs=(VMEM_ALL, ANY, ANY),
+        scratch_shapes=[pltpu.VMEM((rows, hd), F32)] * 3
+        + [
+            pltpu.SemaphoreType.DMA((2, count)),
+            pltpu.SemaphoreType.DMA((2, 2, per)),
+        ],
+        compiler_params=pltpu.CompilerParams(
+            collective_id=number, has_side_effects=True, vmem_limit_bytes=16 << 20
+        ),
         cost_estimate=pl.CostEstimate(
             flops=4 * rows * hd * 5120,
             bytes_accessed=4 << 20,
@@ -497,9 +490,14 @@
     length = lengths[0]
     cache = cache[0, 0]
     cache_other = swap(cache)
-    mix_attn, wide_attn, normed_attn = connect(streams, hc_static[0], hc_dynamic[0])
+    head_rows = gather_rows(jnp.concatenate([w_qkv[:, 0, :], w_out], axis=1), rep_index)
+    qkv_rows, out_rows = head_rows[:, : 3 * head_dim], head_rows[:, 3 * head_dim :]
+    streams = with_layout_constraint(
+        jnp.transpose(streams, (1, 0, 2)), Layout(major_to_minor=(0, 1, 2))
+    )
+    streams = lax.optimization_barrier(streams)
+    mix_attn, normed_attn = connect(streams, hc_static[0], hc_dynamic[0])
     input_attn = gather_tokens(normed_attn, 0).reshape(tok_rep, width)
-    qkv_rows = gather_rows(w_qkv[:, 0, :], rep_index)
     projected = jnp.dot(input_attn, qkv_rows, preferred_element_type=F32)
     row_ids = jnp.arange(tok_rep, dtype=jnp.int32)
     stretch_ids = (row_ids // tok_dev * rep_count + rep_index) * tok_dev + row_ids % tok_dev
@@ -509,15 +507,15 @@
     value_new = projected[:, 2 * head_dim :].astype(BF)
     fresh = jnp.concatenate([key_new, value_new], axis=1)
     fresh_other = swap(fresh)
-    meta = jnp.stack([length, rep_index])
-    attended = attend(meta, queries, cache, cache_other, fresh, fresh_other)
-    out_rows = gather_rows(w_out, rep_index)
+    attended, decode_cache, decode_new = attend(
+        lengths, queries, cache, cache_other, fresh, fresh_other, 4
+    )
     attn_partial = lax.dot_general(
         attended, out_rows, (((1,), (1,)), ((), ())), preferred_element_type=F32
     ).astype(BF)
     attn_branch = scatter_sum(attn_partial.reshape(col_count, tok_dev, width), 1)
-    streams_mid = blend(mix_attn, wide_attn, attn_branch)
-    mix_ffn, wide_ffn, normed_ffn = connect(streams_mid, hc_static[1], hc_dynamic[1])
+    streams_mid = blend(mix_attn, streams, attn_branch)
+    mix_ffn, normed_ffn = connect(streams_mid, hc_static[1], hc_dynamic[1])
     input_ffn = gather_tokens(normed_ffn, 2).reshape(tok_rep, width)
     gate_rows = gather_rows(w_gate_up, rep_index)
     down_rows = gather_rows(w_down, rep_index)
@@ -527,8 +525,7 @@
         hidden, down_rows, (((1,), (1,)), ((), ())), preferred_element_type=F32
     ).astype(BF)
     ffn_branch = scatter_sum(ffn_partial.reshape(col_count, tok_dev, width), 3)
-    new_streams = blend(mix_ffn, wide_ffn, ffn_branch)
-    decode_cache, decode_new = decode_exchange(cache, fresh, 4)
+    new_streams = jnp.transpose(blend(mix_ffn, streams_mid, ffn_branch), (1, 0, 2))
     return (new_streams, decode_cache[None], decode_new[None])
 
 

time: 360 us -> 307 us (0.85)
  the two profiles are of different devices: /device:TPU:34 before, /device:TPU:2 now
where the time goes in v2:
time: 307 us
  Pallas kernels  244 us (79%)
  matrix products  23.5 us (8%)
  between operations  14.8 us (5%)
  local copies, waits for them, and re-layouts  13.3 us (4%)
  other arithmetic  10.8 us (4%)
    pallas_call x2, Pallas kernels, gather_tokens(): pl.pallas_call(gather_kernel, out_shape=jax.ShapeDtypeStruct((NX * NZ, ro...  101 us
    pallas_call x2, Pallas kernels, scatter_sum(): pl.pallas_call(scatter_kernel, out_shape=jax.ShapeDtypeStruct((rows, widt...  96.4 us
    pallas_call x1, Pallas kernels, attend(): pl.pallas_call(attend_kernel, out_shape=(jax.ShapeDtypeStruct((rows, hd),...  46.7 us
    unnamed x37, local copies, waits for them, and re-layouts  12.3 us
    dot_general x1, matrix products, on_device(): jnp.einsum('td,dkf->tkf', input_ffn, gate_rows, preferred_element_type=F32)  9.92 us
  transfers between devices with their start and end apart: 5, of which 0 were waited for; matrix products, arithmetic and copies ran while one was open for 10% of the time, Pallas kernels for 65%

profile of v2, /device:TPU:2, one launch (start us, length us, event | category | flops | bytes accessed | tf_op | source)
XLA Modules:
  0.0 306.5 jit_solution(9953473616611514298)
XLA Ops:
  7.2 1.7 fusion.49
  9.0 0.2 constant_dynamic-slice_fusion.1
  9.2 0.7 copy.36
  10.1 0.6 copy.42
  10.7 0.3 fusion.4
  11.1 0.5 fusion.21
  11.7 2.3 fusion
  14.3 55.1 %gather_tokens.2 = bf16[16,64,2048]{2,1,0:T(8,128)(2,1)S(1)} custom-call(bf16[64,2048]{1,0:T(8,128)(2,1)S(1)} %divide_convert_fusion.1.t_ref), custom_call_target="tpu_custom_call" | custom-call | tf_op jit(solution)/shard_map/gather_tokens/pallas_call | solution.py:158
  69.4 2.0 copy-done.2
  72.1 5.0 %fusion.16 = f32[1024,384]{1,0:T(8,128)S(1)} fusion(bf16[1024,2048]{1,0:T(8,128)(2,1)} %bitcast.93, bf16[2048,512]{1,0:T(8,128)(2,1)} %all-gather.4.cloned.1.call-done), kind=kOutput, calls=%fused_computation.32 | convolution fusion | flops 1610612736 | bytes 7340032 | tf_op jit(solution)/shard_map/dot_general | solution.py:501
  77.1 2.5 fusion.37
  79.7 0.2 pad_maximum_fusion.1.fo_ref
  80.0 0.7 constant_dynamic-slice_fusion
  80.9 1.0 copy-done.4
  81.9 1.3 copy-done.3
  83.2 1.2 copy-done.5
  84.4 46.7 %attend.1 = (bf16[1024,128]{1,0:T(8,128)(2,1)S(1)}, bf16[2,8,128,256]{3,2,1,0:T(8,128)(2,1)S(1)}, bf16[2,8,64,256]{3,2,1,0:T(8,128)(2,1)S(1)}) custom-call(s32[1]{0:T(128)} %copy.45.meta, bf16[1024,128]{1,0:T(8,128)(2,1)S(1)} %pad_maximum_fusion.2.q_ref, bf16[2048,256]{1,0:T(8,128)(2,1)S(1)} %bitcast.97, bf16[2048,256]{1,0:T(8,128)(2,1)S(1)} %copy-done.5, ...), custom_call_target="tpu_custom_call" | custom-call | flops 2684354560 | bytes 4194304 | tf_op jit(solution)/shard_map/attend/pallas_call | solution.py:447
  131.2 2.3 convolution_convert_fusion.1
  133.5 52.4 %scatter_sum.2 = f32[64,2048]{1,0:T(8,128)S(1)} custom-call(bf16[16,64,2048]{2,1,0:T(8,128)(2,1)S(1)} %bitcast.90), custom_call_target="tpu_custom_call" | custom-call | tf_op jit(solution)/shard_map/scatter_sum/pallas_call | solution.py:259
  185.9 0.2 fusion.41
  186.2 0.3 fusion.9
  186.5 0.5 fusion.19
  187.0 2.1 fusion.2
  189.4 45.4 %gather_tokens.3 = bf16[16,64,2048]{2,1,0:T(8,128)(2,1)S(1)} custom-call(bf16[64,2048]{1,0:T(8,128)(2,1)S(1)} %divide_convert_fusion.t_ref), custom_call_target="tpu_custom_call" | custom-call | tf_op jit(solution)/shard_map/gather_tokens/pallas_call | solution.py:158
  234.8 2.0 copy-done.1
  236.8 9.9 %fusion.67 = f32[1024,2,512]{2,0,1:T(8,128)} fusion(bf16[1024,2048,1]{1,0,2:T(8,128)(2,1)} %bitcast.92, bf16[2048,2,512]{2,0,1:T(8,128)(2,1)} %all-gather.6.cloned.1.call-done), kind=kOutput, calls=%fused_computation.131 | convolution fusion | flops 4294967296 | bytes 12582912 | tf_op jit(solution)/shard_map/td,dkf->tkf/dot_general | solution.py:522
  246.7 5.2 %convolution_convert_fusion = bf16[1024,2048]{1,0:T(8,128)(2,1)S(1)} fusion(bf16[2048,512]{1,0:T(8,128)(2,1)} %all-gather.8.cloned.1.call-done, f32[1024,2,512]{2,0,1:T(8,128)} %fusion.67), kind=kOutput, calls=%fused_computation.12 | convolution fusion | flops 2152726528 | bytes 10485760 | tf_op jit(solution)/shard_map/dot_general | solution.py:524
  252.0 44.0 %scatter_sum.3 = f32[64,2048]{1,0:T(8,128)S(1)} custom-call(bf16[16,64,2048]{2,1,0:T(8,128)(2,1)S(1)} %bitcast.91), custom_call_target="tpu_custom_call" | custom-call | tf_op jit(solution)/shard_map/scatter_sum/pallas_call | solution.py:259
  296.1 0.2 fusion.45
  296.5 1.8 copy.32
  298.2 1.0 copy.46
  299.2 0.8 copy.47
  (59 shorter events, 1.5 us)
Async XLA Ops:
  7.2 1.8 copy-start
  7.2 3.0 copy-start.12
  7.2 64.9 %all-gather.4.cloned.1.call-start = ((), (), s32[]{:S(2)}) async-start(), calls=%async_computation | async-start | bytes 2228224 | tf_op jit(solution)/shard_map/all_gather | solution.py:476
  8.9 227.9 %all-gather.6.cloned.1.call-start = ((), (), s32[]{:S(2)}) async-start(), calls=%async_computation.1 | async-start | bytes 4456448 | tf_op jit(solution)/shard_map/all_gather | solution.py:476
  9.2 1.8 copy-start.15
  9.2 1.8 copy-start.13
  10.0 236.7 %all-gather.8.cloned.1.call-start = ((), (), s32[]{:S(2)}) async-start(), calls=%async_computation.2 | async-start | bytes 2228224 | tf_op jit(solution)/shard_map/all_gather | solution.py:476
  10.0 70.9 %collective-permute-start = (bf16[2048,256]{1,0:T(8,128)(2,1)}, bf16[2048,256]{1,0:T(8,128)(2,1)S(1)}, u32[]{:S(2)}, u32[]{:S(2)}) collective-permute-start(bf16[2048,256]{1,0:T(8,128)(2,1)} %bitcast.96), channel_id=1, source_target_pairs={{0,1},{1,0},{2,3},{3,2},{4,5},{5,4},{6,7},{7,6},{8,9},{9,8},{10,11... | collective-permute-start | bytes 3145736 | tf_op jit(solution)/shard_map/ppermute | solution.py:480
  69.4 2.0 copy-start.2
  77.1 2.9 copy-start.14
  79.9 2.0 collective-permute-start.1
  80.9 1.0 copy-start.4
  81.9 1.3 copy-start.3
  83.2 1.2 copy-start.5
  133.5 52.4 %copy-start.6 = (f32[64,2048]{1,0:T(8,128)S(1)}, f32[64,2048]{1,0:T(8,128)}, u32[]{:S(2)}) copy-start(f32[64,2048]{1,0:T(8,128)} %get-tuple-element.23) | copy-start | bytes 1572868
  133.5 52.4 %copy-start.7 = (f32[64,2048]{1,0:T(8,128)S(1)}, f32[64,2048]{1,0:T(8,128)}, u32[]{:S(2)}) copy-start(f32[64,2048]{1,0:T(8,128)} %get-tuple-element.24) | copy-start | bytes 1572868
  133.5 52.4 %copy-start.8 = (f32[64,2048]{1,0:T(8,128)S(1)}, f32[64,2048]{1,0:T(8,128)}, u32[]{:S(2)}) copy-start(f32[64,2048]{1,0:T(8,128)} %get-tuple-element.25) | copy-start | bytes 1572868
  133.5 52.4 %copy-start.9 = (f32[64,2048]{1,0:T(8,128)S(1)}, f32[64,2048]{1,0:T(8,128)}, u32[]{:S(2)}) copy-start(f32[64,2048]{1,0:T(8,128)} %get-tuple-element.26) | copy-start | bytes 1572868
  234.8 2.0 copy-start.1
  252.0 44.1 %copy-start.10 = (f32[64,2048]{1,0:T(8,128)S(1)}, f32[64,2048]{1,0:T(8,128)}, u32[]{:S(2)}) copy-start(f32[64,2048]{1,0:T(8,128)} %get-tuple-element.21) | copy-start | bytes 1572868
  252.0 44.1 %copy-start.11 = (f32[64,2048]{1,0:T(8,128)S(1)}, f32[64,2048]{1,0:T(8,128)}, u32[]{:S(2)}) copy-start(f32[64,2048]{1,0:T(8,128)} %get-tuple-element.22) | copy-start | bytes 1572868
Sparse Core Ops, SparseCore 0:
  10.4 48.4 all-gather.3
  60.7 61.6 all-gather.5
  124.3 35.7 all-gather.7

commit v3 on v2

--- a/solution.py
+++ b/solution.py
@@ -81,73 +81,114 @@
     pl.semaphore_wait(barrier, len(places))
 
 
+def places():
+    x, z, xr, xl, zu, zd = around()
+    x2, z2 = lax.rem(x + 2, NX), lax.rem(z + 2, NZ)
+    return {"x": (x, xr, xl, x2), "zh": (z, zu, zd, z2)}
+
+
+def slot_of(first, i, j):
+    return i * NZ + j if first == "x" else j * NZ + i
+
+
+def neighbours(position):
+    return [{axis: position[axis][step]} for axis in ("x", "zh") for step in (1, 2)]
+
+
+def cut(width):
+    return (0, width - width * 3 // 16), (width - width * 3 // 16, width * 3 // 16)
+
+
+def take_turns(left, right):
+    for _ in left:
+        next(right, None)
+    for _ in right:
+        pass
+
+
 def gather_kernel(t_ref, o_ref, send_sem, recv_sem, own_sem):
-    x, z, xr, xl, zu, zd = around()
-    right, left, up, down = {"x": xr}, {"x": xl}, {"zh": zu}, {"zh": zd}
-    x2, z2 = lax.rem(x + 2, NX), lax.rem(z + 2, NZ)
+    position = places()
     half = t_ref.shape[0] // 2
     top, low = pl.ds(0, half), pl.ds(half, half)
     whole = pl.ds(0, 2 * half)
-    greet((right, left, up, down))
-
-    def copy(kind, src, slot, rows, place):
-        return pltpu.make_async_remote_copy(
-            src_ref=src.at[rows],
-            dst_ref=o_ref.at[slot, rows],
-            send_sem=send_sem.at[kind],
-            recv_sem=recv_sem.at[kind],
-            device_id=place,
-            device_id_type=MESH,
-        )
-
+    mine = position["x"][0] * NZ + position["zh"][0]
+    greet(neighbours(position))
     started = []
 
-    def start(*given):
-        made = copy(*given)
-        made.start()
-        started.append(made)
-
-    mine = x * NZ + z
-
-    def arrived(kind, slot, rows, place):
-        copy(kind, t_ref, slot, rows, place).wait_recv()
-
+    def part(base, first, second, columns):
+        p, pn, pp, p2 = position[first]
+        q, qn, qp, q2 = position[second]
+        right, left, up, down = {second: qn}, {second: qp}, {first: pn}, {first: pp}
+        cols = pl.ds(*columns)
+
+        def at(i, j):
+            return slot_of(first, i, j)
+
+        def copy(kind, own, slot, rows, place):
+            src = t_ref.at[rows, cols] if own else o_ref.at[slot, rows, cols]
+            return pltpu.make_async_remote_copy(
+                src_ref=src,
+                dst_ref=o_ref.at[slot, rows, cols],
+                send_sem=send_sem.at[base + kind],
+                recv_sem=recv_sem.at[base + kind],
+                device_id=place,
+                device_id_type=MESH,
+            )
+
+        def start(*given):
+            made = copy(*given)
+            made.start()
+            started.append(made)
+
+        def arrived(kind, rows, place):
+            copy(kind, True, mine, rows, place).wait_recv()
+
+        start(0, True, mine, whole, up)
+        start(1, True, mine, whole, down)
+        yield
+        start(4, True, mine, whole, right)
+        start(5, True, mine, whole, left)
+        yield
+        below, above, far = at(pp, q), at(pn, q), at(p2, q)
+        arrived(0, whole, up)
+        start(2, False, below, top, up)
+        start(8, False, below, whole, right)
+        start(9, False, below, whole, left)
+        arrived(1, whole, down)
+        start(3, False, above, low, down)
+        start(12, False, above, whole, right)
+        start(13, False, above, whole, left)
+        yield
+        ring = (p, pp, pn, p2)
+
+        def relay(j):
+            arrived(4 + 4 * j, whole, right)
+            start(6 + 4 * j, False, at(ring[j], qp), top, right)
+            arrived(5 + 4 * j, whole, left)
+            start(7 + 4 * j, False, at(ring[j], qn), low, left)
+
+        relay(0)
+        yield
+        arrived(2, top, up)
+        arrived(3, low, down)
+        start(16, False, far, whole, right)
+        start(17, False, far, whole, left)
+        yield
+        for j in range(1, 4):
+            relay(j)
+            yield
+        for j in range(4):
+            arrived(6 + 4 * j, top, right)
+            arrived(7 + 4 * j, low, left)
+
+    most, rest = cut(t_ref.shape[1])
+    along_z = part(0, "zh", "x", most)
+    along_x = part(20, "x", "zh", rest)
+    next(along_x)
+    next(along_z)
     own = pltpu.make_async_copy(t_ref, o_ref.at[mine], own_sem)
-    start(0, t_ref, mine, whole, up)
-    start(1, t_ref, mine, whole, down)
-    start(4, t_ref, mine, whole, right)
-    start(5, t_ref, mine, whole, left)
     own.start()
-    zs = (z, zd, zu, z2)
-    below, above = x * NZ + zd, x * NZ + zu
-    arrived(0, mine, whole, up)
-    start(2, o_ref.at[below], below, top, up)
-    start(8, o_ref.at[below], below, whole, right)
-    start(9, o_ref.at[below], below, whole, left)
-    arrived(1, mine, whole, down)
-    start(3, o_ref.at[above], above, low, down)
-    start(12, o_ref.at[above], above, whole, right)
-    start(13, o_ref.at[above], above, whole, left)
-
-    def relay(j):
-        from_left, from_right = xl * NZ + zs[j], xr * NZ + zs[j]
-        arrived(4 + 4 * j, mine, whole, right)
-        start(6 + 4 * j, o_ref.at[from_left], from_left, top, right)
-        arrived(5 + 4 * j, mine, whole, left)
-        start(7 + 4 * j, o_ref.at[from_right], from_right, low, left)
-
-    relay(0)
-    far = x * NZ + z2
-    arrived(2, mine, top, up)
-    arrived(3, mine, low, down)
-    start(16, o_ref.at[far], far, whole, right)
-    start(17, o_ref.at[far], far, whole, left)
-    relay(1)
-    relay(2)
-    relay(3)
-    for j in range(4):
-        arrived(6 + 4 * j, mine, top, right)
-        arrived(7 + 4 * j, mine, low, left)
+    take_turns(along_z, along_x)
     own.wait()
     for made in started:
         made.wait_send()
@@ -161,8 +202,8 @@
         in_specs=[VMEM_ALL],
         out_specs=VMEM_ALL,
         scratch_shapes=[
-            pltpu.SemaphoreType.DMA((20,)),
-            pltpu.SemaphoreType.DMA((20,)),
+            pltpu.SemaphoreType.DMA((40,)),
+            pltpu.SemaphoreType.DMA((40,)),
             pltpu.SemaphoreType.DMA,
         ],
         compiler_params=pltpu.CompilerParams(
@@ -172,83 +213,114 @@
     )(block)
 
 
-def scatter_kernel(p_ref, o_ref, xin, xsum, tin, total, tsum, send_sem, recv_sem):
-    x, z, xr, xl, zu, zd = around()
-    right, left, up, down = {"x": xr}, {"x": xl}, {"zh": zu}, {"zh": zd}
-    x2, z2 = lax.rem(x + 2, NX), lax.rem(z + 2, NZ)
+def scatter_kernel(p_ref, o_ref, *scratch):
+    send_sem, recv_sem = scratch[-2:]
+    position = places()
     half = p_ref.shape[1] // 2
     top, low = pl.ds(0, half), pl.ds(half, half)
-    greet((right, left, up, down))
+    greet(neighbours(position))
     started = []
-
-    def copy(kind, src, dst, place):
-        return pltpu.make_async_remote_copy(
-            src_ref=src,
-            dst_ref=dst,
-            send_sem=send_sem.at[kind],
-            recv_sem=recv_sem.at[kind],
-            device_id=place,
-            device_id_type=MESH,
-        )
-
-    def start(*given):
-        made = copy(*given)
-        made.start()
-        started.append(made)
-
-    def arrived(kind, ref, place):
-        copy(kind, ref, ref, place).wait_recv()
-
-    zs = (z2, zu, zd, z)
-    for j in range(4):
-        far = x2 * NZ + zs[j]
-        start(6 * j, p_ref.at[far, top], xin.at[j, 0], right)
-        start(6 * j + 1, p_ref.at[far, low], xin.at[j, 1], left)
-    for j in range(4):
-        start(6 * j + 2, p_ref.at[xr * NZ + zs[j], low], xin.at[j, 2], right)
-        start(6 * j + 3, p_ref.at[xl * NZ + zs[j], top], xin.at[j, 3], left)
 
     def wide(ref):
         return ref[...].astype(F32)
 
-    for j in range(4):
-        arrived(6 * j, xin.at[j, 0], right)
-        xsum[j, 0] = (wide(p_ref.at[xr * NZ + zs[j], top]) + wide(xin.at[j, 0])).astype(BF)
-        start(6 * j + 4, xsum.at[j, 0], xin.at[j, 4], right)
-        arrived(6 * j + 1, xin.at[j, 1], left)
-        xsum[j, 1] = (wide(p_ref.at[xl * NZ + zs[j], low]) + wide(xin.at[j, 1])).astype(BF)
-        start(6 * j + 5, xsum.at[j, 1], xin.at[j, 5], left)
-
-    def finish_x(j):
-        for kind, place in ((2, right), (3, left), (4, right), (5, left)):
-            arrived(6 * j + kind, xin.at[j, kind], place)
-        here = x * NZ + zs[j]
-        a = wide(p_ref.at[here, top]) + wide(xin.at[j, 4]) + wide(xin.at[j, 3])
-        b = wide(p_ref.at[here, low]) + wide(xin.at[j, 2]) + wide(xin.at[j, 5])
-        return a, b
-
-    base = 24
-    a, b = finish_x(0)
-    total[0, 0], total[0, 1] = a.astype(BF), b.astype(BF)
-    start(base, total.at[0, 0], tin.at[0], up)
-    start(base + 1, total.at[0, 1], tin.at[1], down)
-    a, b = finish_x(1)
-    total[1, 1] = b.astype(BF)
-    start(base + 2, total.at[1, 1], tin.at[2], up)
-    arrived(base, tin.at[0], up)
-    tsum[0] = (a + wide(tin.at[0])).astype(BF)
-    start(base + 4, tsum.at[0], tin.at[4], up)
-    a, b = finish_x(2)
-    total[2, 0] = a.astype(BF)
-    start(base + 3, total.at[2, 0], tin.at[3], down)
-    arrived(base + 1, tin.at[1], down)
-    tsum[1] = (b + wide(tin.at[1])).astype(BF)
-    start(base + 5, tsum.at[1], tin.at[5], down)
-    a, b = finish_x(3)
-    for kind, place in ((2, up), (3, down), (4, up), (5, down)):
-        arrived(base + kind, tin.at[kind], place)
-    o_ref[top] = a + wide(tin.at[4]) + wide(tin.at[3])
-    o_ref[low] = b + wide(tin.at[2]) + wide(tin.at[5])
+    def part(base, first, second, columns, xin, xsum, tin, total, tsum):
+        p, pn, pp, p2 = position[first]
+        q, qn, qp, q2 = position[second]
+        right, left, up, down = {first: pn}, {first: pp}, {second: qn}, {second: qp}
+        cols = pl.ds(*columns)
+        ring = (q2, qn, qp, q)
+
+        def term(i, j, rows):
+            return p_ref.at[slot_of(first, i, ring[j]), rows, cols]
+
+        def copy(kind, src, dst, place):
+            return pltpu.make_async_remote_copy(
+                src_ref=src,
+                dst_ref=dst,
+                send_sem=send_sem.at[base + kind],
+                recv_sem=recv_sem.at[base + kind],
+                device_id=place,
+                device_id_type=MESH,
+            )
+
+        def start(*given):
+            made = copy(*given)
+            made.start()
+            started.append(made)
+
+        def arrived(kind, ref, place):
+            copy(kind, ref, ref, place).wait_recv()
+
+        def distant(j):
+            start(6 * j, term(p2, j, top), xin.at[j, 0], right)
+            start(6 * j + 1, term(p2, j, low), xin.at[j, 1], left)
+
+        def near(j):
+            start(6 * j + 2, term(pn, j, low), xin.at[j, 2], right)
+            start(6 * j + 3, term(pp, j, top), xin.at[j, 3], left)
+
+        def pass_on(j):
+            arrived(6 * j, xin.at[j, 0], right)
+            xsum[j, 0] = (wide(term(pn, j, top)) + wide(xin.at[j, 0])).astype(BF)
+            start(6 * j + 4, xsum.at[j, 0], xin.at[j, 4], right)
+            arrived(6 * j + 1, xin.at[j, 1], left)
+            xsum[j, 1] = (wide(term(pp, j, low)) + wide(xin.at[j, 1])).astype(BF)
+            start(6 * j + 5, xsum.at[j, 1], xin.at[j, 5], left)
+            if j < 2:
+                distant(j + 2)
+            if j < 3:
+                near(j + 1)
+
+        def finish(j):
+            for kind, place in ((2, right), (3, left), (4, right), (5, left)):
+                arrived(6 * j + kind, xin.at[j, kind], place)
+            a = wide(term(p, j, top)) + wide(xin.at[j, 4]) + wide(xin.at[j, 3])
+            b = wide(term(p, j, low)) + wide(xin.at[j, 2]) + wide(xin.at[j, 5])
+            return a, b
+
+        last = 24
+        distant(0)
+        distant(1)
+        near(0)
+        yield
+        pass_on(0)
+        yield
+        pass_on(1)
+        yield
+        a, b = finish(0)
+        total[0, 0], total[0, 1] = a.astype(BF), b.astype(BF)
+        start(last, total.at[0, 0], tin.at[0], up)
+        start(last + 1, total.at[0, 1], tin.at[1], down)
+        yield
+        pass_on(2)
+        yield
+        a, b = finish(1)
+        total[1, 1] = b.astype(BF)
+        start(last + 2, total.at[1, 1], tin.at[2], up)
+        arrived(last, tin.at[0], up)
+        tsum[0] = (a + wide(tin.at[0])).astype(BF)
+        start(last + 4, tsum.at[0], tin.at[4], up)
+        yield
+        pass_on(3)
+        yield
+        a, b = finish(2)
+        total[2, 0] = a.astype(BF)
+        start(last + 3, total.at[2, 0], tin.at[3], down)
+        arrived(last + 1, tin.at[1], down)
+        tsum[1] = (b + wide(tin.at[1])).astype(BF)
+        start(last + 5, tsum.at[1], tin.at[5], down)
+        yield
+        a, b = finish(3)
+        for kind, place in ((2, up), (3, down), (4, up), (5, down)):
+            arrived(last + kind, tin.at[kind], place)
+        o_ref[top, cols] = a + wide(tin.at[4]) + wide(tin.at[3])
+        o_ref[low, cols] = b + wide(tin.at[2]) + wide(tin.at[5])
+
+    most, rest = cut(p_ref.shape[2])
+    take_turns(
+        part(0, "x", "zh", most, *scratch[:5]), part(30, "zh", "x", rest, *scratch[5:10])
+    )
     for made in started:
         made.wait_send()
 
@@ -256,20 +328,17 @@
 def scatter_sum(partial, number):
     blocks, rows, width = partial.shape
     half = rows // 2
+    buffers = []
+    for first, size in cut(width):
+        for lead in ((4, 6), (4, 2), (6,), (3, 2), (2,)):
+            buffers.append(pltpu.VMEM(lead + (half, size), BF))
     return pl.pallas_call(
         scatter_kernel,
         out_shape=jax.ShapeDtypeStruct((rows, width), F32),
         in_specs=[VMEM_ALL],
         out_specs=VMEM_ALL,
-        scratch_shapes=[
-            pltpu.VMEM((4, 6, half, width), BF),
-            pltpu.VMEM((4, 2, half, width), BF),
-            pltpu.VMEM((6, half, width), BF),
-            pltpu.VMEM((3, 2, half, width), BF),
-            pltpu.VMEM((2, half, width), BF),
-            pltpu.SemaphoreType.DMA((30,)),
-            pltpu.SemaphoreType.DMA((30,)),
-        ],
+        scratch_shapes=buffers
+        + [pltpu.SemaphoreType.DMA((60,)), pltpu.SemaphoreType.DMA((60,))],
         compiler_params=pltpu.CompilerParams(
             collective_id=number, has_side_effects=True, vmem_limit_bytes=48 << 20
         ),

time: 307 us -> 290 us (0.945)
  the two profiles are of different devices: /device:TPU:2 before, /device:TPU:34 now
where the time goes in v3:
time: 290 us
  Pallas kernels  227 us (78%)
  matrix products  23.5 us (8%)
  between operations  14.8 us (5%)
  local copies, waits for them, and re-layouts  13.5 us (5%)
  other arithmetic  10.8 us (4%)
    pallas_call x2, Pallas kernels, gather_tokens(): pl.pallas_call(gather_kernel, out_shape=jax.ShapeDtypeStruct((NX * NZ, ro...  88.1 us
    pallas_call x2, Pallas kernels, scatter_sum(): pl.pallas_call(scatter_kernel, out_shape=jax.ShapeDtypeStruct((rows, widt...  81.9 us
    pallas_call x1, Pallas kernels, attend(): pl.pallas_call(attend_kernel, out_shape=(jax.ShapeDtypeStruct((rows, hd),...  57.1 us
    unnamed x37, local copies, waits for them, and re-layouts  12.4 us
    dot_general x1, matrix products, on_device(): jnp.einsum('td,dkf->tkf', input_ffn, gate_rows, preferred_element_type=F32)  9.92 us
  transfers between devices with their start and end apart: 5, of which 0 were waited for; matrix products, arithmetic and copies ran while one was open for 10% of the time, Pallas kernels for 65%

profile of v3, /device:TPU:34, one launch (start us, length us, event | category | flops | bytes accessed | tf_op | source)
XLA Modules:
  0.0 290.1 jit_solution(18444806471411161211)
XLA Ops:
  7.2 1.7 fusion.49
  9.0 0.2 constant_dynamic-slice_fusion.1
  9.2 0.7 copy.36
  10.1 0.6 copy.42
  10.7 0.3 fusion.4
  11.1 0.5 fusion.21
  11.7 2.3 fusion
  14.3 45.0 %gather_tokens.2 = bf16[16,64,2048]{2,1,0:T(8,128)(2,1)S(1)} custom-call(bf16[64,2048]{1,0:T(8,128)(2,1)S(1)} %divide_convert_fusion.1.t_ref), custom_call_target="tpu_custom_call" | custom-call | tf_op jit(solution)/shard_map/gather_tokens/pallas_call | solution.py:199
  59.3 2.0 copy-done.2
  62.0 5.0 %fusion.16 = f32[1024,384]{1,0:T(8,128)S(1)} fusion(bf16[1024,2048]{1,0:T(8,128)(2,1)} %bitcast.93, bf16[2048,512]{1,0:T(8,128)(2,1)} %all-gather.4.cloned.1.call-done), kind=kOutput, calls=%fused_computation.32 | convolution fusion | flops 1610612736 | bytes 7340032 | tf_op jit(solution)/shard_map/dot_general | solution.py:570
  67.0 2.5 fusion.37
  69.6 0.2 pad_maximum_fusion.1.fo_ref
  69.9 0.7 constant_dynamic-slice_fusion
  70.8 1.0 copy-done.4
  71.8 1.2 copy-done.3
  73.1 1.4 copy-done.5
  74.5 57.1 %attend.1 = (bf16[1024,128]{1,0:T(8,128)(2,1)S(1)}, bf16[2,8,128,256]{3,2,1,0:T(8,128)(2,1)S(1)}, bf16[2,8,64,256]{3,2,1,0:T(8,128)(2,1)S(1)}) custom-call(s32[1]{0:T(128)} %copy.45.meta, bf16[1024,128]{1,0:T(8,128)(2,1)S(1)} %pad_maximum_fusion.2.q_ref, bf16[2048,256]{1,0:T(8,128)(2,1)S(1)} %bitcast.97, bf16[2048,256]{1,0:T(8,128)(2,1)S(1)} %copy-done.5, ...), custom_call_target="tpu_custom_call" | custom-call | flops 2684354560 | bytes 4194304 | tf_op jit(solution)/shard_map/attend/pallas_call | solution.py:516
  131.6 2.3 convolution_convert_fusion.1
  134.0 44.6 %scatter_sum.2 = f32[64,2048]{1,0:T(8,128)S(1)} custom-call(bf16[16,64,2048]{2,1,0:T(8,128)(2,1)S(1)} %bitcast.90), custom_call_target="tpu_custom_call" | custom-call | tf_op jit(solution)/shard_map/scatter_sum/pallas_call | solution.py:335
  178.6 0.2 fusion.41
  178.9 0.3 fusion.9
  179.2 0.5 fusion.19
  179.7 2.1 fusion.2
  182.1 43.1 %gather_tokens.3 = bf16[16,64,2048]{2,1,0:T(8,128)(2,1)S(1)} custom-call(bf16[64,2048]{1,0:T(8,128)(2,1)S(1)} %divide_convert_fusion.t_ref), custom_call_target="tpu_custom_call" | custom-call | tf_op jit(solution)/shard_map/gather_tokens/pallas_call | solution.py:199
  225.1 2.0 copy-done.1
  227.1 9.9 %fusion.67 = f32[1024,2,512]{2,0,1:T(8,128)} fusion(bf16[1024,2048,1]{1,0,2:T(8,128)(2,1)} %bitcast.92, bf16[2048,2,512]{2,0,1:T(8,128)(2,1)} %all-gather.6.cloned.1.call-done), kind=kOutput, calls=%fused_computation.131 | convolution fusion | flops 4294967296 | bytes 12582912 | tf_op jit(solution)/shard_map/td,dkf->tkf/dot_general | solution.py:591
  237.0 5.2 %convolution_convert_fusion = bf16[1024,2048]{1,0:T(8,128)(2,1)S(1)} fusion(bf16[2048,512]{1,0:T(8,128)(2,1)} %all-gather.8.cloned.1.call-done, f32[1024,2,512]{2,0,1:T(8,128)} %fusion.67), kind=kOutput, calls=%fused_computation.12 | convolution fusion | flops 2152726528 | bytes 10485760 | tf_op jit(solution)/shard_map/dot_general | solution.py:593
  242.3 37.3 %scatter_sum.3 = f32[64,2048]{1,0:T(8,128)S(1)} custom-call(bf16[16,64,2048]{2,1,0:T(8,128)(2,1)S(1)} %bitcast.91), custom_call_target="tpu_custom_call" | custom-call | tf_op jit(solution)/shard_map/scatter_sum/pallas_call | solution.py:335
  279.6 0.2 fusion.45
  280.0 1.8 copy.32
  281.8 1.0 copy.46
  282.8 0.8 copy.47
  (59 shorter events, 1.5 us)
Async XLA Ops:
  7.2 1.8 copy-start
  7.2 3.0 %copy-start.12 = (bf16[64,4,2048]{2,1,0:T(4,128)(2,1)S(1)}, bf16[64,4,2048]{2,1,0:T(4,128)(2,1)}, u32[]{:S(2)}) copy-start(bf16[64,4,2048]{2,1,0:T(4,128)(2,1)} %param.9) | copy-start | bytes 3145732
  7.2 54.8 %all-gather.4.cloned.1.call-start = ((), (), s32[]{:S(2)}) async-start(), calls=%async_computation | async-start | bytes 2228224 | tf_op jit(solution)/shard_map/all_gather | solution.py:545
  8.9 218.2 %all-gather.6.cloned.1.call-start = ((), (), s32[]{:S(2)}) async-start(), calls=%async_computation.1 | async-start | bytes 4456448 | tf_op jit(solution)/shard_map/all_gather | solution.py:545
  9.2 1.8 copy-start.15
  9.2 1.8 copy-start.13
  10.0 227.0 %all-gather.8.cloned.1.call-start = ((), (), s32[]{:S(2)}) async-start(), calls=%async_computation.2 | async-start | bytes 2228224 | tf_op jit(solution)/shard_map/all_gather | solution.py:545
  10.0 60.8 %collective-permute-start = (bf16[2048,256]{1,0:T(8,128)(2,1)}, bf16[2048,256]{1,0:T(8,128)(2,1)S(1)}, u32[]{:S(2)}, u32[]{:S(2)}) collective-permute-start(bf16[2048,256]{1,0:T(8,128)(2,1)} %bitcast.96), channel_id=1, source_target_pairs={{0,1},{1,0},{2,3},{3,2},{4,5},{5,4},{6,7},{7,6},{8,9},{9,8},{10,11... | collective-permute-start | bytes 3145736 | tf_op jit(solution)/shard_map/ppermute | solution.py:549
  59.3 2.0 copy-start.2
  67.0 2.9 %copy-start.14 = (bf16[256,512]{1,0:T(8,128)(2,1)S(1)}, bf16[256,512]{1,0:T(8,128)(2,1)}, u32[]{:S(2)}) copy-start(bf16[256,512]{1,0:T(8,128)(2,1)} %param.17) | copy-start | bytes 786436
  69.8 2.0 collective-permute-start.1
  70.8 1.0 copy-start.4
  71.8 1.2 copy-start.3
  73.1 1.4 copy-start.5
  133.9 44.7 %copy-start.6 = (f32[64,2048]{1,0:T(8,128)S(1)}, f32[64,2048]{1,0:T(8,128)}, u32[]{:S(2)}) copy-start(f32[64,2048]{1,0:T(8,128)} %get-tuple-element.23) | copy-start | bytes 1572868
  133.9 44.7 %copy-start.7 = (f32[64,2048]{1,0:T(8,128)S(1)}, f32[64,2048]{1,0:T(8,128)}, u32[]{:S(2)}) copy-start(f32[64,2048]{1,0:T(8,128)} %get-tuple-element.24) | copy-start | bytes 1572868
  133.9 44.7 %copy-start.8 = (f32[64,2048]{1,0:T(8,128)S(1)}, f32[64,2048]{1,0:T(8,128)}, u32[]{:S(2)}) copy-start(f32[64,2048]{1,0:T(8,128)} %get-tuple-element.25) | copy-start | bytes 1572868
  133.9 44.7 %copy-start.9 = (f32[64,2048]{1,0:T(8,128)S(1)}, f32[64,2048]{1,0:T(8,128)}, u32[]{:S(2)}) copy-start(f32[64,2048]{1,0:T(8,128)} %get-tuple-element.26) | copy-start | bytes 1572868
  225.1 2.0 copy-start.1
  242.3 37.4 %copy-start.10 = (f32[64,2048]{1,0:T(8,128)S(1)}, f32[64,2048]{1,0:T(8,128)}, u32[]{:S(2)}) copy-start(f32[64,2048]{1,0:T(8,128)} %get-tuple-element.21) | copy-start | bytes 1572868
  242.3 37.4 %copy-start.11 = (f32[64,2048]{1,0:T(8,128)S(1)}, f32[64,2048]{1,0:T(8,128)}, u32[]{:S(2)}) copy-start(f32[64,2048]{1,0:T(8,128)} %get-tuple-element.22) | copy-start | bytes 1572868
Sparse Core Ops, SparseCore 0:
  10.4 49.0 all-gather.3
  61.4 64.4 all-gather.5
  127.7 53.5 all-gather.7

commit v4 on v3

--- a/solution.py
+++ b/solution.py
@@ -346,7 +346,9 @@
     )(partial)
 
 
-def decode_copies(c_ref, f_ref, dc_ref, dn_ref, send_sem, recv_sem):
+def decode_copies(
+    c_ref, f_ref, dc_ref, dn_ref, c_relay, f_relay, send_sem, recv_sem, pass_sem, relay_sem
+):
     x, z, e = lax.axis_index("x"), lax.axis_index("zh"), lax.axis_index("core")
     col = x * NZ + z
     count = NX * NZ
@@ -354,48 +356,63 @@
     crows, frows = dc_ref.shape[2], dn_ref.shape[2]
     to_core, slot = col // per, lax.rem(col, per)
     barrier = pltpu.get_barrier_semaphore()
-
-    def at(c, core):
-        return {"x": c // NZ, "zh": lax.rem(c, NZ), "core": core}
-
-    for s in range(per):
-        source = e * per + lax.rem(slot + s, per)
+    outs, relays = (dc_ref, dn_ref), (c_relay, f_relay)
+
+    def greet_at(place):
+        pl.semaphore_signal(barrier, inc=1, device_id=place, device_id_type=MESH)
+
+    for s in range(1, count):
+        c = lax.rem(col + s, count)
         for core in range(2):
-
-            @pl.when(jnp.logical_not(jnp.logical_and(source == col, e == core)))
-            def _():
-                pl.semaphore_signal(
-                    barrier, inc=1, device_id=at(source, core), device_id_type=MESH
-                )
-
-    stays = (to_core == e).astype(jnp.int32)
-    pl.semaphore_wait(barrier, count - stays)
-
-    def pieces(c):
-        return (
-            (c_ref.at[pl.ds(pl.multiple_of(c * crows, crows), crows)], dc_ref.at[e, slot]),
-            (f_ref.at[pl.ds(pl.multiple_of(c * frows, frows), frows)], dn_ref.at[e, slot]),
-        )
-
-    def remote(s, kind):
-        c = lax.rem(col + s, count)
-        src, dst = pieces(c)[kind]
+            greet_at({"x": c // NZ, "zh": lax.rem(c, NZ), "core": core})
+    greet_at({"core": 1 - e})
+    pl.semaphore_wait(barrier, 2 * count - 1)
+
+    def piece(kind, c):
+        ref, size = ((c_ref, crows), (f_ref, frows))[kind]
+        return ref.at[pl.ds(pl.multiple_of(c * size, size), size)]
+
+    def remote(kind, dx, dz):
+        tx, tz = lax.rem(x + dx, NX), lax.rem(z + dz, NZ)
+        src = piece(kind, tx * NZ + tz)
+        if dz == 2:
+            via = lax.rem(z + (1 if dx % 2 == 0 else NZ - 1), NZ)
+            dst, arrival = relays[kind].at[dx], relay_sem.at[kind, dx]
+            place = {"x": tx, "zh": via, "core": e}
+        else:
+            dst, arrival = outs[kind].at[e, slot], recv_sem.at[kind, e, slot]
+            place = {"x": tx, "zh": tz, "core": to_core}
         return pltpu.make_async_remote_copy(
             src_ref=src,
             dst_ref=dst,
-            send_sem=send_sem.at[kind, s],
-            recv_sem=recv_sem.at[kind, e, slot],
-            device_id=at(c, to_core),
+            send_sem=send_sem.at[kind, dx * NZ + dz],
+            recv_sem=arrival,
+            device_id=place,
             device_id_type=MESH,
         )
 
+    def onward(kind, dx):
+        step = 1 if dx % 2 == 0 else NZ - 1
+        source = lax.rem(x + NX - dx, NX) * NZ + lax.rem(z + NZ - step, NZ)
+        there = lax.rem(source, per)
+        return pltpu.make_async_remote_copy(
+            src_ref=relays[kind].at[dx],
+            dst_ref=outs[kind].at[e, there],
+            send_sem=pass_sem.at[kind, dx],
+            recv_sem=recv_sem.at[kind, e, there],
+            device_id={"x": x, "zh": lax.rem(z + step, NZ), "core": source // per},
+            device_id_type=MESH,
+        )
+
     def local(kind):
-        src, dst = pieces(col)[kind]
-        return pltpu.make_async_copy(src, dst, send_sem.at[kind, 0])
-
-    for s in range(1, count):
+        return pltpu.make_async_copy(
+            piece(kind, col), outs[kind].at[e, slot], send_sem.at[kind, 0]
+        )
+
+    order = [(dx, dz) for dz in (2, 1, 3, 0) for dx in range(NX) if (dx, dz) != (0, 0)]
+    for dx, dz in order:
         for kind in range(2):
-            remote(s, kind).start()
+            remote(kind, dx, dz).start()
     for kind in range(2):
 
         @pl.when(to_core == e)
@@ -404,12 +421,17 @@
 
         @pl.when(to_core != e)
         def _():
-            remote(0, kind).start()
-
+            remote(kind, 0, 0).start()
+
+    yield
+    for dx in range(NX):
+        for kind in range(2):
+            remote(kind, dx, 2).wait_recv()
+            onward(kind, dx).start()
     yield
     for core in range(2):
         for i in range(per):
-            for kind, ref in ((0, dc_ref), (1, dn_ref)):
+            for kind, ref in enumerate(outs):
 
                 @pl.when(jnp.logical_not(jnp.logical_and(core == e, e * per + i == col)))
                 def _():
@@ -418,14 +440,15 @@
                         dst_ref=ref.at[core, i],
                         send_sem=send_sem.at[kind, 0],
                         recv_sem=recv_sem.at[kind, core, i],
-                        device_id=at(col, 1 - e),
+                        device_id={"core": 1 - e},
                         device_id_type=MESH,
                     ).wait_recv()
 
-    for s in range(1, count):
-        for kind in range(2):
-            remote(s, kind).wait_send()
     for kind in range(2):
+        for dx, dz in order:
+            remote(kind, dx, dz).wait_send()
+        for dx in range(NX):
+            onward(kind, dx).wait_send()
 
         @pl.when(to_core == e)
         def _():
@@ -433,7 +456,7 @@
 
         @pl.when(to_core != e)
         def _():
-            remote(0, kind).wait_send()
+            remote(kind, 0, 0).wait_send()
 
 
 SUB = 256
@@ -441,14 +464,20 @@
 
 
 def attend_kernel(
-    meta, q_ref, co_ref, cx_ref, fo_ref, fx_ref, o_ref, dc_ref, dn_ref,
-    m_ref, l_ref, acc_ref, send_sem, recv_sem,
+    meta, q_ref, c_ref, cx_in, fo_ref, fx_ref, o_ref, dc_ref, dn_ref,
+    m_ref, l_ref, acc_ref, co_ref, cx_ref, load_sem, *scratch,
 ):
     hd = q_ref.shape[1]
     subs = q_ref.shape[0] // SUB
     gain = 1.0 / (math.sqrt(hd) * math.log(2.0))
     length, rep = meta[0], lax.axis_index("core")
-    copies = decode_copies(co_ref, fo_ref, dc_ref, dn_ref, send_sem, recv_sem)
+    loads = [
+        pltpu.make_async_copy(c_ref, co_ref, load_sem.at[0]),
+        pltpu.make_async_copy(cx_in, cx_ref, load_sem.at[1]),
+    ]
+    for load in loads:
+        load.start()
+    copies = decode_copies(c_ref, fo_ref, dc_ref, dn_ref, *scratch)
     next(copies)
     m_ref[...] = jnp.full_like(m_ref, NEGATIVE)
     l_ref[...] = jnp.zeros_like(l_ref)
@@ -484,9 +513,6 @@
 
         lax.fori_loop(0, ref.shape[0] // KEYS, one, 0)
 
-    reach = co_ref.shape[0]
-    cached(co_ref, rep * reach)
-    cached(cx_ref, (1 - rep) * reach)
     tok = meta_tok(q_ref.shape[0])
     row = lax.broadcasted_iota(jnp.int32, (SUB, SUB), 0)
     column = lax.broadcasted_iota(jnp.int32, (SUB, SUB), 1)
@@ -499,6 +525,12 @@
                 absorb(
                     sub, ref[rows, :hd], ref[rows, hd:], allowed if sub == number else None
                 )
+    reach = co_ref.shape[0]
+    loads[0].wait()
+    cached(co_ref, rep * reach)
+    next(copies)
+    loads[1].wait()
+    cached(cx_ref, (1 - rep) * reach)
     o_ref[...] = (acc_ref[...] / l_ref[...]).astype(o_ref.dtype)
     for _ in copies:
         pass
@@ -520,12 +552,18 @@
             jax.ShapeDtypeStruct((2, per, crows // count, width), BF),
             jax.ShapeDtypeStruct((2, per, frows // count, width), BF),
         ),
-        in_specs=[pl.BlockSpec(memory_space=pltpu.SMEM)] + [VMEM_ALL] * 5,
+        in_specs=[pl.BlockSpec(memory_space=pltpu.SMEM), VMEM_ALL, ANY, ANY, VMEM_ALL, VMEM_ALL],
         out_specs=(VMEM_ALL, ANY, ANY),
         scratch_shapes=[pltpu.VMEM((rows, hd), F32)] * 3
+        + [pltpu.VMEM((crows, width), BF)] * 2
         + [
+            pltpu.SemaphoreType.DMA((2,)),
+            pltpu.VMEM((NX, crows // count, width), BF),
+            pltpu.VMEM((NX, frows // count, width), BF),
             pltpu.SemaphoreType.DMA((2, count)),
             pltpu.SemaphoreType.DMA((2, 2, per)),
+            pltpu.SemaphoreType.DMA((2, NX)),
+            pltpu.SemaphoreType.DMA((2, NX)),
         ],
         compiler_params=pltpu.CompilerParams(
             collective_id=number, has_side_effects=True, vmem_limit_bytes=16 << 20

time: 290 us -> 289 us (level)
  Pallas kernels: 227 us -> 224 us
  transfers between devices with their start and end apart: 5 -> 5, of which waited for: 0 -> 0; matrix products, arithmetic and copies ran while one was open for 10% -> 10% of each run, Pallas kernels for 65% -> 66%
where the time goes in v4:
time: 289 us; the launch traced here: 287 us
  Pallas kernels  224 us (78%)
  matrix products  23.5 us (8%)
  between operations  14.8 us (5%)
  local copies, waits for them, and re-layouts  13.5 us (5%)
  other arithmetic  10.8 us (4%)
    pallas_call x2, Pallas kernels, gather_tokens(): pl.pallas_call(gather_kernel, out_shape=jax.ShapeDtypeStruct((NX * NZ, ro...  89.8 us
    pallas_call x2, Pallas kernels, scatter_sum(): pl.pallas_call(scatter_kernel, out_shape=jax.ShapeDtypeStruct((rows, widt...  79.6 us
    pallas_call x1, Pallas kernels, attend(): pl.pallas_call(attend_kernel, out_shape=(jax.ShapeDtypeStruct((rows, hd),...  55 us
    unnamed x37, local copies, waits for them, and re-layouts  12.4 us
    dot_general x1, matrix products, on_device(): jnp.einsum('td,dkf->tkf', input_ffn, gate_rows, preferred_element_type=F32)  9.92 us
  transfers between devices with their start and end apart: 5, of which 0 were waited for; matrix products, arithmetic and copies ran while one was open for 10% of the time, Pallas kernels for 66%

profile of v4, /device:TPU:34, one launch (start us, length us, event | category | flops | bytes accessed | tf_op | source)
XLA Modules:
  0.0 287.5 jit_solution(1018043541522722770)
XLA Ops:
  7.2 1.7 fusion.49
  9.0 0.2 constant_dynamic-slice_fusion.1
  9.2 0.7 copy.36
  10.1 0.6 copy.42
  10.7 0.3 fusion.4
  11.1 0.5 fusion.21
  11.7 2.3 fusion
  14.3 45.0 %gather_tokens.2 = bf16[16,64,2048]{2,1,0:T(8,128)(2,1)S(1)} custom-call(bf16[64,2048]{1,0:T(8,128)(2,1)S(1)} %divide_convert_fusion.1.t_ref), custom_call_target="tpu_custom_call" | custom-call | tf_op jit(solution)/shard_map/gather_tokens/pallas_call | solution.py:199
  59.3 2.0 copy-done.2
  62.0 5.0 %fusion.16 = f32[1024,384]{1,0:T(8,128)S(1)} fusion(bf16[1024,2048]{1,0:T(8,128)(2,1)} %bitcast.93, bf16[2048,512]{1,0:T(8,128)(2,1)} %all-gather.4.cloned.1.call-done), kind=kOutput, calls=%fused_computation.32 | convolution fusion | flops 1610612736 | bytes 7340032 | tf_op jit(solution)/shard_map/dot_general | solution.py:608
  67.0 2.5 fusion.37
  69.6 0.2 pad_maximum_fusion.1.fo_ref
  69.9 0.7 constant_dynamic-slice_fusion
  70.8 1.0 copy-done.4
  71.8 1.2 copy-done.3
  73.1 1.4 copy-done.5
  74.5 55.0 %attend.1 = (bf16[1024,128]{1,0:T(8,128)(2,1)S(1)}, bf16[2,8,128,256]{3,2,1,0:T(8,128)(2,1)S(1)}, bf16[2,8,64,256]{3,2,1,0:T(8,128)(2,1)S(1)}) custom-call(s32[1]{0:T(128)} %copy.45.meta, bf16[1024,128]{1,0:T(8,128)(2,1)S(1)} %pad_maximum_fusion.2.q_ref, bf16[2048,256]{1,0:T(8,128)(2,1)S(1)} %bitcast.97, bf16[2048,256]{1,0:T(8,128)(2,1)S(1)} %copy-done.5, ...), custom_call_target="tpu_custom_call" | custom-call | flops 2684354560 | bytes 4194304 | tf_op jit(solution)/shard_map/attend/pallas_call | solution.py:548
  129.5 2.3 convolution_convert_fusion.1
  131.9 45.1 %scatter_sum.2 = f32[64,2048]{1,0:T(8,128)S(1)} custom-call(bf16[16,64,2048]{2,1,0:T(8,128)(2,1)S(1)} %bitcast.90), custom_call_target="tpu_custom_call" | custom-call | tf_op jit(solution)/shard_map/scatter_sum/pallas_call | solution.py:335
  177.0 0.2 fusion.41
  177.3 0.3 fusion.9
  177.6 0.5 fusion.19
  178.1 2.1 fusion.2
  180.5 44.8 %gather_tokens.3 = bf16[16,64,2048]{2,1,0:T(8,128)(2,1)S(1)} custom-call(bf16[64,2048]{1,0:T(8,128)(2,1)S(1)} %divide_convert_fusion.t_ref), custom_call_target="tpu_custom_call" | custom-call | tf_op jit(solution)/shard_map/gather_tokens/pallas_call | solution.py:199
  225.3 2.0 copy-done.1
  227.2 9.9 %fusion.67 = f32[1024,2,512]{2,0,1:T(8,128)} fusion(bf16[1024,2048,1]{1,0,2:T(8,128)(2,1)} %bitcast.92, bf16[2048,2,512]{2,0,1:T(8,128)(2,1)} %all-gather.6.cloned.1.call-done), kind=kOutput, calls=%fused_computation.131 | convolution fusion | flops 4294967296 | bytes 12582912 | tf_op jit(solution)/shard_map/td,dkf->tkf/dot_general | solution.py:629
  237.2 5.2 %convolution_convert_fusion = bf16[1024,2048]{1,0:T(8,128)(2,1)S(1)} fusion(bf16[2048,512]{1,0:T(8,128)(2,1)} %all-gather.8.cloned.1.call-done, f32[1024,2,512]{2,0,1:T(8,128)} %fusion.67), kind=kOutput, calls=%fused_computation.12 | convolution fusion | flops 2152726528 | bytes 10485760 | tf_op jit(solution)/shard_map/dot_general | solution.py:631
  242.4 34.5 %scatter_sum.3 = f32[64,2048]{1,0:T(8,128)S(1)} custom-call(bf16[16,64,2048]{2,1,0:T(8,128)(2,1)S(1)} %bitcast.91), custom_call_target="tpu_custom_call" | custom-call | tf_op jit(solution)/shard_map/scatter_sum/pallas_call | solution.py:335
  277.0 0.2 fusion.45
  277.4 1.8 copy.32
  279.2 1.0 copy.46
  280.1 0.8 copy.47
  (59 shorter events, 1.5 us)
Async XLA Ops:
  7.2 1.8 copy-start
  7.2 3.0 %copy-start.12 = (bf16[64,4,2048]{2,1,0:T(4,128)(2,1)S(1)}, bf16[64,4,2048]{2,1,0:T(4,128)(2,1)}, u32[]{:S(2)}) copy-start(bf16[64,4,2048]{2,1,0:T(4,128)(2,1)} %param.9) | copy-start | bytes 3145732
  7.2 54.8 %all-gather.4.cloned.1.call-start = ((), (), s32[]{:S(2)}) async-start(), calls=%async_computation | async-start | bytes 2228224 | tf_op jit(solution)/shard_map/all_gather | solution.py:583
  8.9 218.3 %all-gather.6.cloned.1.call-start = ((), (), s32[]{:S(2)}) async-start(), calls=%async_computation.1 | async-start | bytes 4456448 | tf_op jit(solution)/shard_map/all_gather | solution.py:583
  9.2 1.8 copy-start.15
  9.2 1.8 copy-start.13
  10.0 227.2 %all-gather.8.cloned.1.call-start = ((), (), s32[]{:S(2)}) async-start(), calls=%async_computation.2 | async-start | bytes 2228224 | tf_op jit(solution)/shard_map/all_gather | solution.py:583
  10.0 60.8 %collective-permute-start = (bf16[2048,256]{1,0:T(8,128)(2,1)}, bf16[2048,256]{1,0:T(8,128)(2,1)S(1)}, u32[]{:S(2)}, u32[]{:S(2)}) collective-permute-start(bf16[2048,256]{1,0:T(8,128)(2,1)} %bitcast.96), channel_id=1, source_target_pairs={{0,1},{1,0},{2,3},{3,2},{4,5},{5,4},{6,7},{7,6},{8,9},{9,8},{10,11... | collective-permute-start | bytes 3145736 | tf_op jit(solution)/shard_map/ppermute | solution.py:587
  59.3 2.0 copy-start.2
  67.0 2.9 %copy-start.14 = (bf16[256,512]{1,0:T(8,128)(2,1)S(1)}, bf16[256,512]{1,0:T(8,128)(2,1)}, u32[]{:S(2)}) copy-start(bf16[256,512]{1,0:T(8,128)(2,1)} %param.17) | copy-start | bytes 786436
  69.8 2.0 collective-permute-start.1
  70.8 1.0 copy-start.4
  71.8 1.2 copy-start.3
  73.1 1.4 copy-start.5
  131.8 45.2 %copy-start.6 = (f32[64,2048]{1,0:T(8,128)S(1)}, f32[64,2048]{1,0:T(8,128)}, u32[]{:S(2)}) copy-start(f32[64,2048]{1,0:T(8,128)} %get-tuple-element.23) | copy-start | bytes 1572868
  131.8 45.2 %copy-start.7 = (f32[64,2048]{1,0:T(8,128)S(1)}, f32[64,2048]{1,0:T(8,128)}, u32[]{:S(2)}) copy-start(f32[64,2048]{1,0:T(8,128)} %get-tuple-element.24) | copy-start | bytes 1572868
  131.8 45.2 %copy-start.8 = (f32[64,2048]{1,0:T(8,128)S(1)}, f32[64,2048]{1,0:T(8,128)}, u32[]{:S(2)}) copy-start(f32[64,2048]{1,0:T(8,128)} %get-tuple-element.25) | copy-start | bytes 1572868
  131.9 45.2 %copy-start.9 = (f32[64,2048]{1,0:T(8,128)S(1)}, f32[64,2048]{1,0:T(8,128)}, u32[]{:S(2)}) copy-start(f32[64,2048]{1,0:T(8,128)} %get-tuple-element.26) | copy-start | bytes 1572868
  225.3 2.0 copy-start.1
  242.4 34.6 %copy-start.10 = (f32[64,2048]{1,0:T(8,128)S(1)}, f32[64,2048]{1,0:T(8,128)}, u32[]{:S(2)}) copy-start(f32[64,2048]{1,0:T(8,128)} %get-tuple-element.21) | copy-start | bytes 1572868
  242.4 34.6 %copy-start.11 = (f32[64,2048]{1,0:T(8,128)S(1)}, f32[64,2048]{1,0:T(8,128)}, u32[]{:S(2)}) copy-start(f32[64,2048]{1,0:T(8,128)} %get-tuple-element.22) | copy-start | bytes 1572868
Sparse Core Ops, SparseCore 0:
  10.4 49.0 all-gather.3
  61.4 66.7 all-gather.5
  130.0 51.1 all-gather.7
